TPU v7x, 32 devices: a whole 2x2x4 slice. The times are simulated.
32 devices in a mesh: dp: 16 (over z, y, x), head: 2 (over core).
Axes of the slice: x: 2, y: 2, z: 4, core: 2. Of those that a mesh axis runs over, the one named last changes fastest.
Arguments:
- tokens: bfloat16 [8192, 768], P(('dp', 'head')), may hold values from -6 to 6
- w_query: float32 [768, 768], P('dp', 'head'), may hold values from -0.3125 to 0.3125
- w_key: float32 [768, 768], P('dp', 'head'), may hold values from -0.3125 to 0.3125
- w_value: float32 [768, 768], P('dp', 'head'), may hold values from -0.21875 to 0.21875
- w_out: float32 [768, 768], P(('dp', 'head')), may hold values from -0.875 to 0.875
- gain_attn: float32 [768], P(('dp', 'head')), may hold values from 0.5 to 1.5
- bias_attn: float32 [768], P(('dp', 'head')), may hold values from -0.5 to 0.5
- w_up: float32 [768, 3072], P(None, ('dp', 'head')), may hold values from -0.21875 to 0.21875
- w_down: float32 [3072, 768], P(('dp', 'head')), may hold values from -0.109375 to 0.109375
- gain_ffn: float32 [768], P(('dp', 'head')), may hold values from 0.5 to 1.5
- bias_ffn: float32 [768], P(('dp', 'head')), may hold values from -0.5 to 0.5
- seq_lengths: int32 [16, 8], P('dp'), may hold values from 0 to 512, as said below
- seq_offsets: int32 [16, 8], P('dp'), may hold values from 0 to 512, as said below
- out_grad: bfloat16 [8192, 768], P(('dp', 'head')), may hold values from -6 to 6
Outputs:
- output: bfloat16 [8192, 768], P(('dp', 'head'))
- input_grad: bfloat16 [8192, 768], P(('dp', 'head'))
- grad_w_query: float32 [768, 768], P('dp', 'head')
- grad_w_key: float32 [768, 768], P('dp', 'head')
- grad_w_value: float32 [768, 768], P('dp', 'head')
- grad_w_out: float32 [768, 768], P(('dp', 'head'))
- grad_gain_attn: float32 [768], P(('dp', 'head'))
- grad_bias_attn: float32 [768], P(('dp', 'head'))
- grad_w_up: float32 [768, 3072], P(None, ('dp', 'head'))
- grad_w_down: float32 [3072, 768], P(('dp', 'head'))
- grad_gain_ffn: float32 [768], P(('dp', 'head'))
- grad_bias_ffn: float32 [768], P(('dp', 'head'))
Inputs may be any that keep to these rules, and one draw needn't show every extreme that they name: Slot j of bin b holds a sequence of seq_lengths[b, j] rows, 0 marking an empty slot; the lengths of a bin sum to at most 512. The sequence in slot j of bin b takes rows seq_offsets[b, j] to seq_offsets[b, j] + seq_lengths[b, j] - 1 of that bin; the sequences of a bin do not intersect; rows that no sequence takes are padding.
All inputs are finite; a program needn't handle non-finite values.
Results may differ from a plain program's by a relative error of at most 0.017.
The roundings to bfloat16 on the way count: a program that leaves them out, or rounds other values in their place, can miss the bound.
Values may be sent and summed in bfloat16 or wider, within the bound.
A program may use at most 128 MiB of HBM per device.

v0:
```python
import math

import jax
import jax.numpy as jnp
from jax import lax
from jax.sharding import PartitionSpec as P

HD = 64
BIN = 512


epsilon = 1e-12


def labels_of(lengths, offsets):
    position = jnp.arange(BIN, dtype=jnp.int32)[:, None]
    starts = offsets[None, :]
    inside = (position >= starts) & (position < starts + lengths[None, :])
    slot_order = jnp.arange(1, lengths.shape[0] + 1, dtype=jnp.int32)[None, :]
    return jnp.sum(jnp.where(inside, slot_order, 0), axis=1)


def layer_norm(operand, gain_vec, bias_vec):
    row_mean = jnp.mean(operand, axis=-1, keepdims=True)
    centered = operand - row_mean
    inverse = lax.rsqrt(jnp.mean(centered * centered, axis=-1, keepdims=True) + epsilon)
    normed = centered * inverse
    return (normed * gain_vec + bias_vec, normed, inverse)


def norm_back(grad_rows, normed, inverse, gain_vec):
    scaled = grad_rows * gain_vec
    inner = jnp.mean(scaled * normed, axis=-1, keepdims=True)
    return inverse * (scaled - jnp.mean(scaled, axis=-1, keepdims=True) - normed * inner)


def gelu_exact(operand):
    return jax.nn.gelu(operand, approximate=False)


def contract_rows(left, right):
    return lax.dot_general(
        left, right, (((0,), (0,)), ((), ())), preferred_element_type=jnp.float32
    )


def contract_cols(left, right):
    return lax.dot_general(
        left, right, (((1,), (1,)), ((), ())), preferred_element_type=jnp.float32
    )


def score_block(queries, key_rows, labels_bin, factor):
    scores = (
        jnp.einsum("qhd,khd->hqk", queries, key_rows, preferred_element_type=jnp.float32) * factor
    )
    allowed = ((labels_bin[:, None] == labels_bin[None, :]) & (labels_bin[:, None] > 0))[None]
    live_rows = (labels_bin > 0)[None, :, None]
    return (scores, allowed, live_rows)


def masked_exp(scores, allowed, row_top):
    return jnp.where(allowed, jnp.exp(jnp.where(allowed, scores - row_top, 0.0)), 0.0)


def attend_bin(pieces, factor):
    queries, key_rows, value_rows, labels_bin = pieces
    scores, allowed, live_rows = score_block(queries, key_rows, labels_bin, factor)
    row_top = jnp.max(jnp.where(allowed, scores, -1e30), axis=2, keepdims=True)
    row_top = jnp.where(live_rows, row_top, 0.0)
    weights = masked_exp(scores, allowed, row_top)
    denominator = jnp.sum(weights, axis=2, keepdims=True) + jnp.where(live_rows, 0.0, 1.0)
    probability = (weights / denominator).astype(jnp.bfloat16)
    mixed_rows = jnp.einsum(
        "hqk,khd->qhd", probability, value_rows, preferred_element_type=jnp.float32
    )
    return (mixed_rows.astype(jnp.bfloat16), row_top, denominator)


def attend_back(pieces, factor):
    queries, key_rows, value_rows, labels_bin, row_top, denominator, grad_mixed = pieces
    scores, allowed, live_rows = score_block(queries, key_rows, labels_bin, factor)
    probability = masked_exp(scores, allowed, row_top) / denominator
    grad_values = jnp.einsum(
        "hqk,qhd->khd",
        probability.astype(jnp.bfloat16),
        grad_mixed,
        preferred_element_type=jnp.float32,
    )
    grad_probs = jnp.einsum(
        "qhd,khd->hqk", grad_mixed, value_rows, preferred_element_type=jnp.float32
    )
    row_delta = jnp.sum(probability * grad_probs, axis=2, keepdims=True)
    grad_scores = (probability * (grad_probs - row_delta)).astype(jnp.bfloat16)
    grad_queries = (
        jnp.einsum("hqk,khd->qhd", grad_scores, key_rows, preferred_element_type=jnp.float32)
        * factor
    )
    grad_keys = (
        jnp.einsum("hqk,qhd->khd", grad_scores, queries, preferred_element_type=jnp.float32)
        * factor
    )
    return (
        grad_queries.astype(jnp.bfloat16),
        grad_keys.astype(jnp.bfloat16),
        grad_values.astype(jnp.bfloat16),
    )


def per_device(
    tokens,
    w_query,
    w_key,
    w_value,
    w_out,
    gain_attn,
    bias_attn,
    w_up,
    w_down,
    gain_ffn,
    bias_ffn,
    seq_lengths,
    seq_offsets,
    out_grad,
):
    low_type = jnp.bfloat16
    bin_count = seq_lengths.shape[0]
    group_rows = bin_count * BIN
    head_width = w_query.shape[1]
    local_heads = head_width // HD
    factor = 1.0 / math.sqrt(HD)
    labels = jax.vmap(labels_of)(seq_lengths, seq_offsets)
    full_query, full_key, full_value = (
        lax.all_gather(w_query.astype(low_type), "dp", axis=0, tiled=True),
        lax.all_gather(w_key.astype(low_type), "dp", axis=0, tiled=True),
        lax.all_gather(w_value.astype(low_type), "dp", axis=0, tiled=True),
    )
    projection = jnp.concatenate([full_query, full_key, full_value], axis=1)
    whole_rows = lax.all_gather(tokens, "head", axis=0, tiled=True)
    projected = jnp.dot(whole_rows, projection, preferred_element_type=jnp.float32).astype(low_type)
    shape_bins = (bin_count, BIN, local_heads, HD)
    queries = projected[:, :head_width].reshape(shape_bins)
    key_rows = projected[:, head_width : 2 * head_width].reshape(shape_bins)
    value_rows = projected[:, 2 * head_width :].reshape(shape_bins)
    mixed_bins, row_tops, denominators = lax.map(
        lambda pieces: attend_bin(pieces, factor), (queries, key_rows, value_rows, labels)
    )
    attended = mixed_bins.reshape(group_rows, head_width)
    out_full, up_part, down_part, gain_one, bias_one, gain_two, bias_two = (
        lax.all_gather(w_out.astype(low_type), ("dp", "head"), axis=0, tiled=True),
        lax.all_gather(w_up.astype(low_type), ("dp", "head"), axis=1, tiled=True),
        lax.all_gather(w_down.astype(low_type), ("dp", "head"), axis=0, tiled=True),
        lax.all_gather(gain_attn.astype(low_type), ("dp", "head"), axis=0, tiled=True),
        lax.all_gather(bias_attn.astype(low_type), ("dp", "head"), axis=0, tiled=True),
        lax.all_gather(gain_ffn.astype(low_type), ("dp", "head"), axis=0, tiled=True),
        lax.all_gather(bias_ffn.astype(low_type), ("dp", "head"), axis=0, tiled=True),
    )
    gain_first = gain_one.astype(jnp.float32)
    gain_second = gain_two.astype(jnp.float32)
    token_view = lax.all_to_all(attended, "head", split_axis=0, concat_axis=1, tiled=True)
    first_sum = tokens.astype(jnp.float32) + jnp.dot(
        token_view, out_full, preferred_element_type=jnp.float32
    )
    normed_one, unit_one, inverse_one = layer_norm(
        first_sum, gain_first, bias_one.astype(jnp.float32)
    )
    ffn_input = normed_one.astype(low_type)
    pre_act = jnp.dot(ffn_input, up_part, preferred_element_type=jnp.float32)
    activated, gelu_pull = jax.vjp(gelu_exact, pre_act)
    hidden = activated.astype(low_type)
    second_sum = normed_one + jnp.dot(hidden, down_part, preferred_element_type=jnp.float32)
    result, unit_two, inverse_two = layer_norm(
        second_sum, gain_second, bias_two.astype(jnp.float32)
    )
    output = result.astype(low_type)
    grad_result = out_grad.astype(jnp.float32)
    grad_gain_two = jnp.sum(grad_result * unit_two, axis=0)
    grad_bias_two = jnp.sum(grad_result, axis=0)
    grad_second = norm_back(grad_result, unit_two, inverse_two, gain_second)
    grad_ffn = grad_second.astype(low_type)
    grad_down_part = contract_rows(hidden, grad_ffn)
    grad_pre = gelu_pull(contract_cols(grad_ffn, down_part))[0].astype(low_type)
    grad_up_part = contract_rows(ffn_input, grad_pre)
    grad_normed = grad_second + contract_cols(grad_pre, up_part)
    grad_gain_one = jnp.sum(grad_normed * unit_one, axis=0)
    grad_bias_one = jnp.sum(grad_normed, axis=0)
    grad_first = norm_back(grad_normed, unit_one, inverse_one, gain_first)
    grad_branch = grad_first.astype(low_type)
    grad_out_full = contract_rows(token_view, grad_branch)
    part_out, part_up, part_down, part_gain_one, part_bias_one, part_gain_two, part_bias_two = (
        lax.psum_scatter(grad_out_full, ("dp", "head"), scatter_dimension=0, tiled=True),
        lax.psum_scatter(grad_up_part, ("dp", "head"), scatter_dimension=1, tiled=True),
        lax.psum_scatter(grad_down_part, ("dp", "head"), scatter_dimension=0, tiled=True),
        lax.psum_scatter(grad_gain_one, ("dp", "head"), scatter_dimension=0, tiled=True),
        lax.psum_scatter(grad_bias_one, ("dp", "head"), scatter_dimension=0, tiled=True),
        lax.psum_scatter(grad_gain_two, ("dp", "head"), scatter_dimension=0, tiled=True),
        lax.psum_scatter(grad_bias_two, ("dp", "head"), scatter_dimension=0, tiled=True),
    )
    grad_token_view = contract_cols(grad_branch, out_full).astype(low_type)
    grad_attended = lax.all_to_all(grad_token_view, "head", split_axis=1, concat_axis=0, tiled=True)
    grad_bins = grad_attended.reshape(shape_bins)
    grad_queries, grad_keys, grad_values = lax.map(
        lambda pieces: attend_back(pieces, factor),
        (queries, key_rows, value_rows, labels, row_tops, denominators, grad_bins),
    )
    grad_projected = jnp.concatenate(
        [
            grad_queries.reshape(group_rows, head_width),
            grad_keys.reshape(group_rows, head_width),
            grad_values.reshape(group_rows, head_width),
        ],
        axis=1,
    )
    grad_projection = contract_rows(whole_rows, grad_projected)
    part_query, part_key, part_value = (
        lax.psum_scatter(grad_projection[:, :head_width], "dp", scatter_dimension=0, tiled=True),
        lax.psum_scatter(
            grad_projection[:, head_width : 2 * head_width], "dp", scatter_dimension=0, tiled=True
        ),
        lax.psum_scatter(
            grad_projection[:, 2 * head_width :], "dp", scatter_dimension=0, tiled=True
        ),
    )
    input_grad = (
        grad_first
        + lax.psum_scatter(
            contract_cols(grad_projected, projection).astype(jnp.bfloat16),
            "head",
            scatter_dimension=0,
            tiled=True,
        ).astype(jnp.float32)
    ).astype(low_type)
    return (
        output,
        input_grad,
        part_query,
        part_key,
        part_value,
        part_out,
        part_gain_one,
        part_bias_one,
        part_up,
        part_down,
        part_gain_two,
        part_bias_two,
    )


def solution(mesh):
    return jax.shard_map(
        per_device,
        mesh=mesh,
        in_specs=(
            P(("dp", "head"), None),
            P("dp", "head"),
            P("dp", "head"),
            P("dp", "head"),
            P(("dp", "head"), None),
            P(("dp", "head")),
            P(("dp", "head")),
            P(None, ("dp", "head")),
            P(("dp", "head"), None),
            P(("dp", "head")),
            P(("dp", "head")),
            P("dp", None),
            P("dp", None),
            P(("dp", "head"), None),
        ),
        out_specs=(
            P(("dp", "head"), None),
            P(("dp", "head"), None),
            P("dp", "head"),
            P("dp", "head"),
            P("dp", "head"),
            P(("dp", "head"), None),
            P(("dp", "head")),
            P(("dp", "head")),
            P(None, ("dp", "head")),
            P(("dp", "head"), None),
            P(("dp", "head")),
            P(("dp", "head")),
        ),
        check_vma=False,
    )
```

profile of v0, /device:TPU:0, one launch (start us, length us, event | category | flops | bytes accessed | tf_op | source)
XLA Modules:
  0.0 1045.2 jit_solution(3644172747977620570)
XLA Ops:
  7.2 1.5 convert_element_type.131
  8.8 1.6 convert_element_type.137
  10.5 1.7 convert_element_type.139
  12.2 0.9 convert_element_type.123
  13.1 0.9 convert_element_type.124
  14.0 0.9 convert_element_type.125
  14.9 0.7 bitcast_add_fusion
  15.6 0.7 select_reduce_fusion.1
  16.3 46.0 %all_gather.33 = bf16[768,384]{1,0:T(8,128)(2,1)S(1)} all-gather(bf16[48,384]{1,0:T(8,128)(2,1)S(1)} %convert_element_type.123), channel_id=1, replica_groups=mesh['dp'=16,'head'=2] {'dp'}, dimensions={0}, use_global_device_ids=true | all-gather | bytes 626688 | tf_op jit(solution)/shard_map/all_gather | solution.py:134
  62.4 40.7 %all_gather.34 = bf16[768,384]{1,0:T(8,128)(2,1)S(1)} all-gather(bf16[48,384]{1,0:T(8,128)(2,1)S(1)} %convert_element_type.124), channel_id=1, replica_groups=mesh['dp'=16,'head'=2] {'dp'}, dimensions={0}, use_global_device_ids=true | all-gather | bytes 626688 | tf_op jit(solution)/shard_map/all_gather | solution.py:135
  103.2 44.1 %all_gather.35 = bf16[768,384]{1,0:T(8,128)(2,1)S(1)} all-gather(bf16[48,384]{1,0:T(8,128)(2,1)S(1)} %convert_element_type.125), channel_id=1, replica_groups=mesh['dp'=16,'head'=2] {'dp'}, dimensions={0}, use_global_device_ids=true | all-gather | bytes 626688 | tf_op jit(solution)/shard_map/all_gather | solution.py:136
  147.5 2.4 all_gather.36
  149.8 0.2 compare_and_fusion
  150.1 1.1 fusion.8
  151.4 1.2 select_reduce_fusion
  152.6 1.5 fusion.1
  154.2 1.1 copy-done
  155.3 2.1 fusion.21
  157.5 0.8 copy.54
  158.3 3.5 all-to-all-start
  161.9 0.2 dynamic-update-slice.1
  162.7 37.8 %all-reduce.9 = (bf16[768]{0:T(1024)(128)(2,1)S(1)}, bf16[768]{0:T(1024)(128)(2,1)S(1)}, bf16[768]{0:T(1024)(128)(2,1)S(1)}, bf16[768]{0:T(1024)(128)(2,1)S(1)}) all-reduce(bf16[768]{0:T(1024)(128)(2,1)S(1)} %dynamic-update-slice.1, bf16[768]{0:T(1024)(128)(2,1)S(1)} %dynamic-update-slice, ...), channel_id=1, replica_groups=mesh['dp'=16,'head'=2] {'dp','head'}, use_global_device_ids=true, to_apply=%add.1 | all-reduce | flops 3072 | bytes 12288
  200.6 2.0 fusion.55
  202.7 0.2 multiply_reduce_fusion.4
  203.0 11.3 %multiply_convert_fusion.1 = (bf16[256,3072]{1,0:T(8,128)(2,1)S(1)}, f32[256,3072]{1,0:T(8,128)}, f32[256,3072]{1,0:T(8,128)}) fusion(bf16[768,3072]{0,1:T(8,128)(2,1)} %all-gather.6.cloned.1.call-done, f32[256,768]{1,0:T(8,128)S(1)} %get-tuple-element.147, f32[768]{0:T(1024)S(1)} %convert_element_type.135, f32[768]{0:T(1024)S(1)} %convert_element_type.133, ...), kind=kOutput, calls=%fused_computation.10 | convolution fusion | flops 1260060672 | bytes 13377536 | tf_op jit(solution)/shard_map/dot_general | solution.py:168
  214.3 4.4 fusion.56
  218.7 0.2 multiply_reduce_fusion.3
  219.0 1.8 fusion.30
  221.0 3.8 add_convert_fusion
  224.9 2.3 multiply_reduce_fusion.1
  227.2 0.9 subtract_multiply_fusion
  228.1 0.5 convolution_convert_fusion.2
  228.7 4.9 all_to_all.35
  233.6 2.0 copy.56
  235.6 2.0 squeeze.36
  237.7 5.2 fusion.18
  242.9 2.7 multiply_reduce_fusion
  245.6 2.1 multiply_convert_fusion
  247.8 1.1 fusion.14
  248.8 0.6 fusion.13
  249.5 2.2 convolution_convert_fusion.1
  251.8 2.1 convolution_bitcast_fusion
  253.9 1.7 fusion.53
  255.5 2.7 copy.67
  258.3 2.7 copy.69
  261.1 1.4 copy.71
  262.7 1.9 fusion.32
  264.6 6.6 fusion.44
  271.3 0.3 reduce-scatter.20.cloned.1.call-start
  271.6 0.8 copy-done.4
  272.5 6.7 fusion.35
  279.3 0.6 copy-done.30
  279.9 42.1 %all-reduce.8 = (f32[768]{0:T(1024)S(1)}, f32[768]{0:T(1024)S(1)}, f32[768]{0:T(1024)S(1)}, f32[768]{0:T(1024)S(1)}) all-reduce(f32[768]{0:T(1024)S(1)} %copy-done.38, f32[768]{0:T(1024)S(1)} %copy-done.39, f32[768]{0:T(1024)S(1)} %copy-done.30, f32[768]{0:T(1024)S(1)} %copy-done.31), channel_id=7, replica_groups=mesh['dp'=16,'head'=2] {'dp','head'}, use_global_device_ids=true, to_apply=%region_18.19.clone | all-reduce | flops 3072 | bytes 24576
  322.1 0.6 dynamic-slice.2
  322.6 0.6 dynamic-slice.3
  323.2 0.6 dynamic-slice.4
  323.8 0.6 dynamic-slice.5
  324.4 1.8 add_convert_fusion.1
  326.2 65.9 %reduce-scatter.22.cloned.1.call-done = f32[48,384]{1,0:T(8,128)} async-done(((f32[768,384]{1,0:T(8,128)}), f32[48,384]{1,0:T(8,128)}) %reduce-scatter.22.cloned.1.call-update) | async-done | bytes 73744
  392.1 129.3 %reduce-scatter.24.cloned.1.call-done = f32[48,384]{1,0:T(8,128)} async-done(((f32[768,384]{1,0:T(8,128)}), f32[48,384]{1,0:T(8,128)}) %reduce-scatter.24.cloned.1.call-update) | async-done | bytes 73744
  521.4 129.4 %reduce-scatter.26.cloned.1.call-done = f32[48,384]{1,0:T(8,128)} async-done(((f32[768,384]{1,0:T(8,128)}), f32[48,384]{1,0:T(8,128)}) %reduce-scatter.26.cloned.1.call-update) | async-done | bytes 73744
  650.7 104.5 %reduce-scatter.16.cloned.1.call-done = f32[24,768]{1,0:T(8,128)} async-done(((f32[768,768]{1,0:T(8,128)}), f32[24,768]{1,0:T(8,128)}) %reduce-scatter.16.cloned.1.call-update) | async-done | bytes 73744 | tf_op jit(solution)/shard_map/reduce_scatter | solution.py:191
  755.2 141.7 %reduce-scatter.18.cloned.1.call-done = f32[768,96]{0,1:T(8,128)} async-done(((f32[768,3072]{0,1:T(8,128)}), f32[768,96]{0,1:T(8,128)}) %reduce-scatter.18.cloned.1.call-update) | async-done | bytes 294928 | tf_op jit(solution)/shard_map/reduce_scatter | solution.py:192
  896.9 141.4 %reduce-scatter.20.cloned.1.call-done = f32[96,768]{1,0:T(8,128)} async-done(((f32[3072,768]{1,0:T(8,128)}), f32[96,768]{1,0:T(8,128)}) %reduce-scatter.20.cloned.1.call-update) | async-done | bytes 294928 | tf_op jit(solution)/shard_map/reduce_scatter | solution.py:193
  (159 shorter events, 2.3 us)
Async XLA Ops:
  7.2 193.5 %all-gather.4.cloned.1.call-start = ((), (), s32[]{:S(2)}) async-start(), calls=%async_computation.9 | async-start | bytes 1216512 | tf_op jit(solution)/shard_map/all_gather | solution.py:150
  8.8 194.2 %all-gather.6.cloned.1.call-start = ((), (), s32[]{:S(2)}) async-start(), calls=%async_computation.10 | async-start | bytes 4866048 | tf_op jit(solution)/shard_map/all_gather | solution.py:151
  10.5 137.0 %copy-start.12 = (bf16[256,768]{1,0:T(8,128)(2,1)S(1)}, bf16[256,768]{1,0:T(8,128)(2,1)}, u32[]{:S(2)}) copy-start(bf16[256,768]{1,0:T(8,128)(2,1)} %param.14) | copy-start | bytes 1179652
  10.5 203.8 %all-gather.8.cloned.1.call-start = ((), (), s32[]{:S(2)}) async-start(), calls=%async_computation.11 | async-start | bytes 4866048 | tf_op jit(solution)/shard_map/all_gather | solution.py:152
  147.5 2.6 copy-start.20
  149.8 1.4 copy-start.15
  151.3 1.2 copy-start.6
  151.3 2.8 copy-start.17
  152.6 2.7 copy-start
  152.6 2.7 copy-start.22
  154.1 3.2 copy-start.24
  155.2 6.5 copy-start.41
  155.2 6.6 copy-start.42
  155.2 6.6 copy-start.43
  155.2 6.6 copy-start.44
  158.3 42.3 %all-to-all-start = ((bf16[2,256,384]{1,2,0:T(8,128)(2,1)}), bf16[2,256,384]{1,2,0:T(8,128)(2,1)S(1)}, u32[]{:S(2)}, u32[]{:S(2)}) async-start(bf16[2,256,384]{1,2,0:T(8,128)(2,1)} %copy.54), calls=%async_computation | async-start | bytes 786432 | tf_op jit(solution)/shard_map/all_to_all | solution.py:160
  161.7 162.7 %reduce-scatter.14.cloned.1.call-start = ((), (), s32[]{:S(2)}) async-start(), calls=%async_computation.12 | async-start | bytes 1179648 | tf_op jit(solution)/shard_map/reduce_scatter | solution.py:226
  200.6 13.6 %copy-start.8 = (bf16[2,256,384]{1,2,0:T(8,128)(2,1)}, bf16[2,256,384]{1,2,0:T(8,128)(2,1)S(1)}, u32[]{:S(2)}) copy-start(bf16[2,256,384]{1,2,0:T(8,128)(2,1)S(1)} %all-to-all-done) | copy-start | bytes 1179652
  202.7 24.5 %copy-start.1 = (f32[256,768]{1,0:T(8,128)}, f32[256,768]{1,0:T(8,128)S(1)}, u32[]{:S(2)}) copy-start(f32[256,768]{1,0:T(8,128)S(1)} %get-tuple-element.147) | copy-start | bytes 2359300
  202.9 21.9 %copy-start.26 = (f32[256]{0:T(256)}, f32[256]{0:T(256)S(1)}, u32[]{:S(2)}) copy-start(f32[256]{0:T(256)S(1)} %add_rsqrt_fusion.1) | copy-start | bytes 3076
  214.3 6.5 copy-start.10
  214.3 4.7 copy-start.13
  214.3 6.5 copy-start.40
  214.3 6.5 copy-start.46
  214.3 6.7 copy-start.47
  218.7 6.1 copy-start.3
  218.7 6.1 copy-start.28
  219.0 5.9 copy-start.32
  219.0 5.9 slice-start.2
  220.8 4.1 copy-start.34
  220.8 4.1 copy-start.36
  221.0 3.9 slice-start.3
  224.9 2.3 copy-start.11
  224.9 3.2 copy-start.5
  228.7 14.1 %slice-start = ((s8[6291456]{0:T(1024)(128)(4,1)}), s8[2097152]{0:T(1024)(128)(4,1)S(1)}, s32[]{:S(2)}) async-start(s8[6291456]{0:T(1024)(128)(4,1)} %bitcast.63), calls=%async_computation.19 | async-start | bytes 4194304
  237.7 5.2 slice-start.1
  237.7 5.2 copy-start.18
  237.7 5.2 copy-start.19
  237.7 5.2 copy-start.23
  237.7 5.2 copy-start.25
  242.9 6.6 copy-start.45
  245.6 2.2 copy-start.7
  247.8 1.7 copy-start.21
  249.5 2.3 copy-start.16
  251.7 140.3 %reduce-scatter.22.cloned.1.call-start = ((), (), s32[]{:S(2)}) async-start(), calls=%async_computation.16 | async-start | bytes 1253376
  258.3 263.1 %reduce-scatter.24.cloned.1.call-start = ((), (), s32[]{:S(2)}) async-start(), calls=%async_computation.17 | async-start | bytes 1253376
  258.3 4.3 copy-start.9
  261.1 389.6 %reduce-scatter.26.cloned.1.call-start = ((), (), s32[]{:S(2)}) async-start(), calls=%async_computation.18 | async-start | bytes 1253376
  262.6 2.0 copy-start.2
  262.6 2.0 copy-start.27
  262.6 492.6 %reduce-scatter.16.cloned.1.call-start = ((), (), s32[]{:S(2)}) async-start(), calls=%async_computation.13 | async-start | bytes 2433024 | tf_op jit(solution)/shard_map/reduce_scatter | solution.py:191
  264.6 632.3 %reduce-scatter.18.cloned.1.call-start = ((), (), s32[]{:S(2)}) async-start(), calls=%async_computation.14 | async-start | bytes 9732096 | tf_op jit(solution)/shard_map/reduce_scatter | solution.py:192
  271.3 1.1 copy-start.4
  271.3 1.2 copy-start.14
  271.3 1.2 copy-start.29
  271.3 1.2 copy-start.33
  271.3 1.2 copy-start.35
  271.3 1.2 copy-start.37
  271.3 767.0 %reduce-scatter.20.cloned.1.call-start = ((), (), s32[]{:S(2)}) async-start(), calls=%async_computation.15 | async-start | bytes 9732096 | tf_op jit(solution)/shard_map/reduce_scatter | solution.py:193
  279.3 0.7 copy-start.30
  279.3 0.7 copy-start.31
  279.3 0.7 copy-start.38
  279.3 0.7 copy-start.39
Sparse Core Ops, SparseCore 0:
  11.5 58.0 all-gather.3
  73.0 65.1 all-gather.5
  141.7 62.3 all-gather.7
  251.8 8.7 reduce-scatter.13
  265.8 126.2 reduce-scatter.21
  397.2 124.0 reduce-scatter.23
  526.7 123.9 reduce-scatter.25
  656.6 98.5 reduce-scatter.15
  761.7 135.1 reduce-scatter.17
  903.2 135.0 reduce-scatter.19
where the time goes:
time: 1050 us
  waiting for transfers between devices  712 us (68%)
  blocking collectives  218 us (21%)
  matrix products  57.8 us (6%)
  local copies, waits for them, and re-layouts  19.9 us (2%)
  other arithmetic  17.9 us (2%)
  between operations  15 us (1%)
    unnamed x13, waiting for transfers between devices  325 us
    reduce_scatter x1, waiting for transfers between devices, per_device(): lax.psum_scatter(grad_up_part, ('dp', 'head'), scatter_dimension=1, tiled...  142 us
    reduce_scatter x1, waiting for transfers between devices, per_device(): lax.psum_scatter(grad_down_part, ('dp', 'head'), scatter_dimension=0, til...  141 us
    reduce_scatter x1, waiting for transfers between devices, per_device(): lax.psum_scatter(grad_out_full, ('dp', 'head'), scatter_dimension=0, tile...  104 us
    unnamed x2, blocking collectives  79.9 us
    all_gather x1, blocking collectives, per_device(): lax.all_gather(w_query.astype(low_type), 'dp', axis=0, tiled=True)  46 us
    all_gather x1, blocking collectives, per_device(): lax.all_gather(w_value.astype(low_type), 'dp', axis=0, tiled=True)  44.1 us
    all_gather x1, blocking collectives, per_device(): lax.all_gather(w_key.astype(low_type), 'dp', axis=0, tiled=True)  40.7 us
  transfers between devices with their start and end apart: 11, of which 6 were waited for; matrix products, arithmetic and copies ran while one was open for 6% of the time, Pallas kernels for 0%

commit v1 on v0

v1 whole, which is shorter than its diff:
```python
import functools
import math
import types

import jax
import jax.numpy as jnp
from jax import lax
from jax.experimental import pallas as pl
from jax.experimental.pallas import tpu as pltpu
from jax.sharding import PartitionSpec as P

HD = 64
BIN = 512
EPS = 1e-12
F32 = jnp.float32
BF = jnp.bfloat16
MESH = pl.DeviceIdType.MESH

MU, MV = 2, 1
ROWS = {"Q": 48, "O": 48, "U": 96, "D": 96}
COLS = {"Q": 1152, "O": 384, "U": 768, "D": 768}
APART = {"Q": 32, "O": 32, "U": 64, "D": 64}
PIECES = ("Q", "O", "U", "D")
PER_PIECE = ("G", "S1", "R1", "S2A", "R2A", "S3A", "R3A", "S2C", "R2C", "S3C", "R3C")
DP, HEAD = "dp", "head"
BOTH = (DP, HEAD)


def mm(a, b, ca=1, cb=0):
    return lax.dot_general(a, b, (((ca,), (cb,)), ((), ())), preferred_element_type=F32)


def scratch_list():
    items = []

    def add(name, shape, dtype):
        items.append((name, pltpu.VMEM(shape, dtype)))

    add("X", (512, 768), BF)
    add("WQ", (768, 1152), BF)
    add("WOP", (2, 768, 384), BF)
    add("WO", (768, 768), BF)
    add("WU", (1536, 768), BF)
    add("WD", (1536, 768), BF)
    for n in ("Q3", "K3", "V3", "ATT", "GA", "DQ", "DK", "DV"):
        add(n, (3, 512, 128), BF)
    add("ATTR", (3, 256, 128), BF)
    add("GAS", (3, 256, 128), BF)
    add("BIAS", (512, 512), F32)
    add("LIVE", (512, 128), F32)
    add("P32", (6, 512, 512), F32)
    add("PB", (512, 512), BF)
    add("DSB", (512, 512), BF)
    add("U1", (256, 768), F32)
    add("N1", (256, 768), F32)
    add("INV1", (256, 128), F32)
    add("FIN", (512, 768), BF)
    add("HID", (4, 512, 384), BF)
    add("GEL", (4, 512, 384), F32)
    add("SEC", (512, 768), F32)
    add("SECR", (256, 768), F32)
    add("GS", (256, 768), F32)
    add("GFB", (512, 768), BF)
    add("GB", (256, 768), BF)
    add("IGS", (256, 768), BF)
    add("IGR", (256, 768), BF)
    add("T", (768, 1152), F32)
    add("S0", (768, 384), BF)
    add("R0", (768, 384), BF)
    for p in PIECES:
        r, c, a = ROWS[p], COLS[p], APART[p]
        b = r - a
        sizes = (8 * r, 8 * r, 8 * r, 4 * a, 4 * a, 3 * a, 3 * a, 6 * b, 6 * b, b, b)
        for key, size in zip(PER_PIECE, sizes):
            add(key + p, (size, c), F32 if key == "G" else BF)
    add("VS", (96, 768), F32)
    add("VR", (80, 768), F32)
    add("UT", (128, 768), F32)
    items.append(("ss", pltpu.SemaphoreType.DMA((320,))))
    items.append(("rs", pltpu.SemaphoreType.DMA((320,))))
    items.append(("ls", pltpu.SemaphoreType.DMA((4,))))
    return items


IN_NAMES = ("tok", "wq", "wk", "wv", "wo", "ga", "ba", "wu", "wd", "gf", "bf", "len", "off", "og")
OUT_NAMES = ("out", "ig", "dwq", "dwk", "dwv", "dwo", "dga", "dba", "dwu", "dwd", "dgf", "dbf")


def layer_kernel(*refs):
    names = IN_NAMES + OUT_NAMES + tuple(n for n, _ in scratch_list())
    named = dict(zip(names, refs))
    r = types.SimpleNamespace(**named)
    for key in PER_PIECE:
        setattr(r, key, {p: named[key + p] for p in PIECES})
    me = lax.axis_index(DP)
    c = lax.axis_index(HEAD)
    x = lax.rem(me, 2)
    y = lax.rem(lax.div(me, 2), 2)
    z = lax.div(me, 4)
    u = x + c * (y - x)
    v = y + c * (x - y)
    ub = 1 + c
    vb = 2 - c
    zs = (z, z + 1 - 2 * lax.rem(z, 2), lax.rem(z + 2, 4), 3 - z)

    def chip(m):
        zm, du, dv = m // 4, (m // 2) % 2, m % 2
        uu = 1 - u if du else u
        vv = 1 - v if dv else v
        return 4 * zs[zm] + ub * uu + vb * vv

    ids = [chip(m) for m in range(16)]
    partner = (me, 1 - c)
    base256, base24, other24 = 256 * c, 24 * c, 24 * (1 - c)
    own_rows = pl.ds(pl.multiple_of(256 * c, 256), 256)
    oth_rows = pl.ds(pl.multiple_of(256 * (1 - c), 256), 256)

    peers = [partner] + [(ids[m], c) for m in (MU, MV, 4, 8, 12)]
    barrier = pltpu.get_barrier_semaphore()
    for dev in peers:
        pl.semaphore_signal(barrier, inc=1, device_id=dev, device_id_type=MESH)
    pl.semaphore_wait(barrier, len(peers))

    sends = []
    recv_ids = {}

    def recv_sem(key):
        if key not in recv_ids:
            recv_ids[key] = len(recv_ids)
        return r.rs.at[recv_ids[key]]

    def send(key, src, dst, dev):
        cp = pltpu.make_async_remote_copy(
            src_ref=src,
            dst_ref=dst,
            send_sem=r.ss.at[len(sends)],
            recv_sem=recv_sem(key),
            device_id=dev,
            device_id_type=MESH,
        )
        cp.start()
        sends.append((src, dst, len(sends), key, dev))

    def wait_send(entry):
        src, dst, k, key, dev = entry
        pltpu.make_async_remote_copy(
            src_ref=src,
            dst_ref=dst,
            send_sem=r.ss.at[k],
            recv_sem=recv_sem(key),
            device_id=dev,
            device_id_type=MESH,
        ).wait_send()

    waited = set()

    def wait_sent(key):
        for entry in sends:
            if entry[3] == key:
                wait_send(entry)
                waited.add(key)

    def wait_recv(key, ref):
        pltpu.make_async_remote_copy(
            src_ref=ref,
            dst_ref=ref,
            send_sem=r.ss.at[0],
            recv_sem=recv_sem(key),
            device_id=partner,
            device_id_type=MESH,
        ).wait_recv()

    def wbuf(p):
        return {"Q": r.WQ, "O": r.WOP.at[c], "U": r.WU, "D": r.WD}[p]

    starts = {}
    for n_rows in (48, 96):
        for m in range(16):
            first = pl.multiple_of(ids[m] * n_rows, 16)
            third = pl.multiple_of(ids[m] * n_rows + 2 * n_rows // 3, 16)
            starts[n_rows, m] = (first, third)

    def wslice(p, part, m):
        a, rows = APART[p], ROWS[p]
        first, third = starts[rows, m]
        if part == "A":
            return wbuf(p).at[pl.ds(first, a), :]
        return wbuf(p).at[pl.ds(third, rows - a), :]

    def forward(p, part, m, f):
        ref = wslice(p, part, m)
        send(("ag", p, part, m ^ f), ref, ref, (ids[f], c))

    def got(p, part, m):
        wait_recv(("ag", p, part, m), wslice(p, part, m))

    def ag_own(p):
        for f in (4, 8, 12):
            forward(p, "A", 0, f)
        forward(p, "C", 0, MU)
        forward(p, "A", 0, MU)
        forward(p, "A", 0, MV)
        for f in (4, 8, 12):
            forward(p, "C", 0, f)
        forward(p, "C", 0, MV)

    def ag_steps(p):
        steps = []

        def step(part, m, flips):
            def run():
                got(p, part, m)
                for f in flips:
                    forward(p, part, m, f)

            steps.append(run)

        step("C", MU, (4, 8, 12, MV))
        step("A", MU, (MV,))
        for zz in (4, 8, 12):
            step("A", zz, (MU, MV))
        for zz in (4, 8, 12):
            step("C", zz, (MV,))
            step("C", zz + MU, (MV,))
        for zz in (4, 8, 12):
            step("A", zz + MU, (MV,))
        return steps

    def ag_plane(p, zm):
        for m in (4 * zm + MV, 4 * zm + MU + MV):
            got(p, "A", m)
            got(p, "C", m)

    def run(steps):
        for s in steps:
            s()

    vec_peer = (partner, (ids[MU], c), (ids[MV], c), (ids[4], c), (ids[8], c))

    def vec_send(k, s):
        send(("v", k, s), r.VS.at[pl.ds(48 * k + 8 * s, 8), :], r.VR.at[pl.ds(40 * k + 8 * s, 8), :], vec_peer[s])

    def vec_step(k, s):
        src, got_row = pl.ds(48 * k + 8 * s, 8), pl.ds(40 * k + 8 * s, 8)
        wait_recv(("v", k, s), r.VR.at[got_row, :])
        r.VS[pl.ds(48 * k + 8 * s + 8, 8), :] = r.VS[src, :] + r.VR[got_row, :]
        if s < 4:
            vec_send(k, s + 1)

    def rs1_send(p, zm):
        rows = 2 * ROWS[p]
        s = pl.ds(zm * rows, rows)
        send(("r1", p, zm), r.S1[p].at[s, :], r.R1[p].at[s, :], (ids[MV], c))

    def rs_sum1(p, zm):
        rows, a = ROWS[p], APART[p]
        b = rows - a
        g, r1 = r.G[p], r.R1[p]
        s = pl.ds(zm * 2 * rows, 2 * rows)
        wait_recv(("r1", p, zm), r1.at[s, :])
        for du in (1, 0):
            o = (2 * zm + du) * rows
            top = g[o : o + a, :] + r1[o : o + a, :].astype(F32)
            low = g[o + a : o + rows, :] + r1[o + a : o + rows, :].astype(F32)
            if du == 1:
                q = pl.ds(zm * a, a)
                r.S2A[p][q, :] = top.astype(BF)
                send(("r2a", p, zm), r.S2A[p].at[q, :], r.R2A[p].at[q, :], (ids[MU], c))
            else:
                g[o : o + a, :] = top
            if zm:
                q = pl.ds(((zm - 1) * 2 + du) * b, b)
                r.S2C[p][q, :] = low.astype(BF)
            else:
                g[o + a : o + rows, :] = low
        if zm:
            q = pl.ds((zm - 1) * 2 * b, 2 * b)
            send(("r2c", p, zm), r.S2C[p].at[q, :], r.R2C[p].at[q, :], (ids[4 * zm], c))

    def rs_sum2a(p, zm):
        rows, a = ROWS[p], APART[p]
        g, r2 = r.G[p], r.R2A[p]
        q = pl.ds(zm * a, a)
        wait_recv(("r2a", p, zm), r2.at[q, :])
        o = 2 * zm * rows
        val = g[o : o + a, :] + r2[q, :].astype(F32)
        if zm:
            k = pl.ds((zm - 1) * a, a)
            r.S3A[p][k, :] = val.astype(BF)
            send(("r3a", p, zm), r.S3A[p].at[k, :], r.R3A[p].at[k, :], (ids[4 * zm], c))
        else:
            g[o : o + a, :] = val

    def rs_sum2c(p):
        rows, a = ROWS[p], APART[p]
        b = rows - a
        g, r2 = r.G[p], r.R2C[p]
        for zm in (1, 2, 3):
            wait_recv(("r2c", p, zm), r2.at[pl.ds((zm - 1) * 2 * b, 2 * b), :])
        for du in (1, 0):
            o = du * rows + a
            val = g[o : o + b, :]
            for zm in (1, 2, 3):
                k = ((zm - 1) * 2 + du) * b
                val = val + r2[k : k + b, :].astype(F32)
            if du == 1:
                r.S3C[p][...] = val.astype(BF)
                send(("r3c", p), r.S3C[p], r.R3C[p], (ids[MU], c))
            else:
                g[o : o + b, :] = val

    def rs_final(p):
        rows, a = ROWS[p], APART[p]
        g = r.G[p]
        r3a, r3c = r.R3A[p], r.R3C[p]
        for zm in (1, 2, 3):
            wait_recv(("r3a", p, zm), r3a.at[pl.ds((zm - 1) * a, a), :])
        val = g[0:a, :]
        for zm in (1, 2, 3):
            val = val + r3a[(zm - 1) * a : zm * a, :].astype(F32)
        g[0:a, :] = val
        wait_recv(("r3c", p), r3c)
        g[a:rows, :] = g[a:rows, :] + r3c[...].astype(F32)

    def block_row(zm, du, dv):
        uu = 1 - u if du else u
        vv = 1 - v if dv else v
        return ub * uu + vb * vv

    def stage(p, zm, src, base):
        rows, cols = ROWS[p], COLS[p]
        for du in (1, 0):
            k = (2 * zm + du) * rows
            far = pl.ds(pl.multiple_of(base + block_row(zm, du, 1) * rows, 8), rows)
            near = pl.ds(pl.multiple_of(base + block_row(zm, du, 0) * rows, 8), rows)
            r.S1[p][k : k + rows, :] = src[far, 0:cols].astype(BF)
            r.G[p][k : k + rows, :] = src[near, 0:cols]
        rs1_send(p, zm)

    r.WQ[pl.ds(pl.multiple_of(me * 48, 16), 48), 0:384] = r.wq[...].astype(BF)
    r.WQ[pl.ds(pl.multiple_of(me * 48, 16), 48), 384:768] = r.wk[...].astype(BF)
    r.WQ[pl.ds(pl.multiple_of(me * 48, 16), 48), 768:1152] = r.wv[...].astype(BF)
    ag_own("Q")
    send("tok", r.tok, r.X.at[own_rows, :], partner)
    local = pltpu.make_async_copy(r.tok, r.X.at[own_rows, :], r.ls.at[0])
    local.start()
    flat = 2 * me + c
    r.VS[0:8, :] = jnp.zeros((8, 768), F32)
    for k, n in enumerate(("ga", "ba", "gf", "bf")):
        r.VS[k : k + 1, 0:24] = getattr(r, n)[...].reshape(1, 24).astype(BF).astype(F32)
    r.VS[0:8, :] = pltpu.roll(r.VS[0:8, :], 24 * flat, 1)
    vec_send(0, 0)
    wo = r.wo[...]
    r.WOP[c, pl.ds(pl.multiple_of(me * 48, 16), 48), :] = jnp.concatenate(
        [wo[:, 0:384], wo[:, 384:768]], axis=0
    ).astype(BF)
    ag_own("O")
    wut = jnp.transpose(jnp.concatenate([r.wu[...], jnp.zeros((768, 32), F32)], axis=1))
    r.WU[pl.ds(pl.multiple_of(me * 96, 16), 96), :] = wut[0:96, :].astype(BF)
    r.WD[pl.ds(pl.multiple_of(me * 96, 16), 96), :] = r.wd[...].astype(BF)

    col_pos = lax.broadcasted_iota(jnp.int32, (512, 128), 0)
    row_pos = lax.broadcasted_iota(jnp.int32, (8, 512), 1)
    col_lab = jnp.zeros((512, 128), jnp.int32)
    row_lab = jnp.zeros((8, 512), jnp.int32)
    for j in range(8):
        lo = r.off[0, j]
        hi = lo + r.len[0, j]
        col_lab = jnp.where((col_pos >= lo) & (col_pos < hi), j + 1, col_lab)
        row_lab = jnp.where((row_pos >= lo) & (row_pos < hi), j + 1, row_lab)
    r.LIVE[...] = jnp.where(col_lab > 0, 1.0, 0.0).astype(F32)
    row_lab = jnp.where(row_lab > 0, row_lab, -1)
    for t in range(4):
        q = slice(128 * t, 128 * t + 128)
        lab = jnp.concatenate([col_lab[q]] * 4, axis=1)
        same = lab == jnp.broadcast_to(row_lab[0:1], (128, 512))
        r.BIAS[q, :] = jnp.where(same, 0.0, -1e30).astype(F32)

    run(ag_steps("Q")[:7])
    ag_own("U")
    run(ag_steps("Q")[7:])
    o_steps, u_steps, d_steps = ag_steps("O"), ag_steps("U"), ag_steps("D")
    vec_step(0, 0)
    wait_recv("tok", r.X.at[own_rows, :])
    local.wait()
    run(o_steps[:4])
    for zm in range(4):
        ag_plane("Q", zm)

    for k, n in enumerate(("Q3", "K3", "V3")):
        full = mm(r.X[...], r.WQ[:, 384 * k : 384 * k + 384])
        full = full.astype(BF)
        if k == 0:
            full = full * BF(0.125)
        for i in range(3):
            getattr(r, n)[i] = full[:, 128 * i : 128 * i + 128]
    ag_own("D")
    vec_step(0, 1)

    for i in range(3):
        r.ATT[i] = jnp.zeros((512, 128), BF)
    fw_hooks = [
        o_steps[4:9],
        o_steps[9:] + u_steps[:1],
        [functools.partial(vec_step, 0, 2)] + u_steps[1:4],
        u_steps[4:7],
        [functools.partial(vec_step, 0, 3)] + u_steps[7:10],
        u_steps[10:],
    ]
    lane = lax.broadcasted_iota(jnp.int32, (1, 128), 1)

    def half(val, a):
        keep = (lane >= 64 * a) & (lane < 64 * a + 64)
        return jnp.where(keep, val, jnp.zeros_like(val))

    def at_index(h, hooks):
        for k, steps in enumerate(hooks):

            def go(steps=steps):
                run(steps)

            pl.when(h == k)(go)

    def fwd_head(h, carry):
        at_index(h, fw_hooks)
        i = lax.div(h, 2)
        a = lax.rem(h, 2)
        vals = half(r.V3[i], a)
        keys = half(r.K3[i], a)
        for t in range(4):
            q = slice(128 * t, 128 * t + 128)
            s = mm(r.Q3[i, q, :], keys, 1, 1) + r.BIAS[q, :]
            live = r.LIVE[q, 0:1]
            top = jnp.where(live > 0, jnp.max(s, axis=1, keepdims=True), 0.0)
            w = jnp.exp(s - top)
            total = jnp.sum(w, axis=1, keepdims=True) + (1.0 - live)
            prob = w * (1.0 / total)
            r.P32[h, q, :] = prob
            o = mm(prob.astype(BF), vals)
            r.ATT[i, q, :] = r.ATT[i, q, :] + o.astype(BF)
        return carry

    lax.fori_loop(0, 6, fwd_head, 0)

    send("att", r.ATT.at[:, oth_rows, :], r.ATTR, partner)
    for zm in range(4):
        ag_plane("O", zm)
    send("wop", r.WOP.at[c], r.WOP.at[c], partner)
    run(d_steps[:4])
    vec_step(0, 4)
    wait_recv("wop", r.WOP.at[1 - c])

    def build_out(i, carry):
        for k in range(2):
            blk = r.WOP[k, pl.ds(pl.multiple_of(48 * i, 16), 48), :].astype(F32)
            rows = jnp.concatenate([blk[0:24], blk[24:48]], axis=1)
            r.T[pl.ds(pl.multiple_of(48 * i + 24 * k, 8), 24), 0:768] = rows
        return carry

    lax.fori_loop(0, 16, build_out, 0)
    r.WO[...] = r.T[:, 0:768].astype(BF)
    wait_recv("att", r.ATTR)
    own_heads = pl.ds(pl.multiple_of(384 * c, 128), 384)
    oth_heads = pl.ds(pl.multiple_of(384 * (1 - c), 128), 384)

    def joined(ref, rows):
        return jnp.concatenate([ref[i, rows, :] for i in range(3)], axis=1)

    all256 = pl.ds(0, 256)
    branch = mm(joined(r.ATT, own_rows), r.WO[own_heads, :])
    branch = branch + mm(joined(r.ATTR, all256), r.WO[oth_heads, :])
    r.GS[...] = branch
    run(d_steps[4:6])

    def norm(val):
        mean = jnp.mean(val, axis=1, keepdims=True)
        cen = val - mean
        inv = lax.rsqrt(jnp.mean(cen * cen, axis=1, keepdims=True) + EPS)
        return cen * inv, inv

    def ln1(t, carry):
        q = pl.ds(pl.multiple_of(64 * t, 64), 64)
        unit, inv = norm(r.tok[q, :].astype(F32) + r.GS[q, :])
        r.U1[q, :] = unit
        r.INV1[q, :] = jnp.broadcast_to(inv, (64, 128))
        one = unit * r.VS[40:41, :] + r.VS[41:42, :]
        r.N1[q, :] = one
        r.FIN[pl.ds(pl.multiple_of(base256 + 64 * t, 64), 64), :] = one.astype(BF)
        return carry

    lax.fori_loop(0, 4, ln1, 0)
    send("fin", r.FIN.at[own_rows, :], r.FIN.at[own_rows, :], partner)
    run(d_steps[6:8])
    wait_recv("fin", r.FIN.at[oth_rows, :])

    def plane_rows(zm):
        return pl.ds(pl.multiple_of(384 * zs[zm], 128), 384)

    def ffn_up(zm):
        for t in range(2):
            q = slice(256 * t, 256 * t + 256)
            pre = mm(r.FIN[q, :], r.WU[plane_rows(zm), :], 1, 1)
            r.GEL[zm, q, :] = pre

        def act(t, carry):
            q = pl.ds(pl.multiple_of(64 * t, 64), 64)
            pre = r.GEL[zm, q, :]
            cdf = 0.5 * (1.0 + lax.erf(pre * (2.0**-0.5)))
            pdf = jnp.exp(-0.5 * pre * pre) * (1.0 / math.sqrt(2.0 * math.pi))
            r.HID[zm, q, :] = (pre * cdf).astype(BF)
            r.GEL[zm, q, :] = cdf + pre * pdf
            return carry

        lax.fori_loop(0, 8, act, 0)

    d_groups = (d_steps[8:10], d_steps[10:12], d_steps[12:], [])
    for zm in range(4):
        ag_plane("U", zm)
        ffn_up(zm)
        run(d_groups[zm])
    for zm in range(4):
        ag_plane("D", zm)
        for rows in (oth_rows, own_rows):
            part = mm(r.HID[zm, rows, :], r.WD[plane_rows(zm), :])
            if zm:
                part = part + r.SEC[rows, :]
            r.SEC[rows, :] = part
            if zm == 3 and rows is oth_rows:
                send("sec", r.SEC.at[oth_rows, :], r.SECR, partner)
    wait_recv("sec", r.SECR)

    def ln2(t, sums):
        dg, db = sums
        q = pl.ds(pl.multiple_of(64 * t, 64), 64)
        qq = pl.ds(pl.multiple_of(base256 + 64 * t, 64), 64)
        unit, inv = norm(r.N1[q, :] + (r.SEC[qq, :] + r.SECR[q, :]))
        gain = r.VS[42:43, :]
        r.out[q, :] = (unit * gain + r.VS[43:44, :]).astype(BF)
        e = r.og[q, :].astype(F32)
        dg = dg + jnp.sum(e * unit, axis=0, keepdims=True)
        db = db + jnp.sum(e, axis=0, keepdims=True)
        eg = e * gain
        inner = jnp.mean(eg * unit, axis=1, keepdims=True)
        gs = inv * (eg - jnp.mean(eg, axis=1, keepdims=True) - unit * inner)
        r.GS[q, :] = gs
        r.GFB[qq, :] = gs.astype(BF)
        return dg, db

    zero = jnp.zeros((1, 768), F32)
    dg2, db2 = lax.fori_loop(0, 4, ln2, (zero, zero))
    send("gfb", r.GFB.at[own_rows, :], r.GFB.at[own_rows, :], partner)
    wait_recv("gfb", r.GFB.at[oth_rows, :])
    wait_sent("sec")

    for n_done, zm in enumerate((3, 2, 1, 0)):
        r.T[0:384, 0:768] = mm(r.HID[zm], r.GFB[...], 0, 0)
        stage("D", zm, r.T, 0)
        for t in range(2):
            q = slice(256 * t, 256 * t + 256)
            gh = mm(r.GFB[q, :], r.WD[plane_rows(zm), :], 1, 1)
            r.HID[zm, q, :] = (gh * r.GEL[zm, q, :]).astype(BF)
        r.T[384:768, 0:768] = mm(r.HID[zm], r.FIN[...], 0, 0)
        stage("U", zm, r.T, 384)
        for rows in (oth_rows, own_rows):
            part = mm(r.HID[zm, rows, :], r.WU[plane_rows(zm), :])
            if n_done:
                part = part + r.SEC[rows, :]
            r.SEC[rows, :] = part
            if n_done == 3 and rows is oth_rows:
                send("gn", r.SEC.at[oth_rows, :], r.SECR, partner)
        if n_done:
            rs_sum1("D", zm + 1)
    wait_recv("gn", r.SECR)

    def ln1_back(t, sums):
        dg, db = sums
        q = pl.ds(pl.multiple_of(64 * t, 64), 64)
        qq = pl.ds(pl.multiple_of(base256 + 64 * t, 64), 64)
        e = r.GS[q, :] + (r.SEC[qq, :] + r.SECR[q, :])
        unit = r.U1[q, :]
        inv = r.INV1[q, 0:1]
        dg = dg + jnp.sum(e * unit, axis=0, keepdims=True)
        db = db + jnp.sum(e, axis=0, keepdims=True)
        eg = e * r.VS[40:41, :]
        inner = jnp.mean(eg * unit, axis=1, keepdims=True)
        first = inv * (eg - jnp.mean(eg, axis=1, keepdims=True) - unit * inner)
        r.GS[q, :] = first
        r.GB[q, :] = first.astype(BF)
        return dg, db

    dg1, db1 = lax.fori_loop(0, 4, ln1_back, (zero, zero))
    r.VS[48:56, :] = jnp.zeros((8, 768), F32)
    for k, val in enumerate((dg1, db1, dg2, db2)):
        r.VS[48 + k : 49 + k, :] = val
    vec_send(1, 0)

    gview = mm(r.GB[...], r.WO[oth_heads, :], 1, 1).astype(BF)
    for i in range(3):
        r.GAS[i] = gview[:, 128 * i : 128 * i + 128]
    send("gas", r.GAS, r.GA.at[:, own_rows, :], partner)
    gview = mm(r.GB[...], r.WO[own_heads, :], 1, 1).astype(BF)
    for i in range(3):
        r.GA[i, own_rows, :] = gview[:, 128 * i : 128 * i + 128]
    rs_sum1("D", 0)
    r.T[own_heads, 0:768] = mm(joined(r.ATT, own_rows), r.GB[...], 0, 0)
    r.T[oth_heads, 0:768] = mm(joined(r.ATTR, all256), r.GB[...], 0, 0)

    def pair_out(i, carry):
        q = pl.ds(pl.multiple_of(48 * i, 16), 48)
        blk = r.T[pl.ds(pl.multiple_of(48 * i + other24, 8), 24), 0:768]
        r.S0[q, :] = jnp.concatenate([blk[:, 0:384], blk[:, 384:768]], axis=0).astype(BF)
        return carry

    lax.fori_loop(0, 16, pair_out, 0)
    send("s0", r.S0, r.R0, partner)
    rs_sum1("U", 3)
    rs_sum1("U", 2)
    wait_recv("s0", r.R0)

    def out_block(m):
        i = ids[m]
        blk = r.T[pl.ds(pl.multiple_of(48 * i + base24, 8), 24), 0:768]
        blk = jnp.concatenate([blk[:, 0:384], blk[:, 384:768]], axis=0)
        return blk + r.R0[pl.ds(pl.multiple_of(48 * i, 16), 48), :].astype(F32)

    for zm in (3, 2, 1, 0):
        for du in (1, 0):
            k = (2 * zm + du) * 48
            r.S1["O"][k : k + 48, :] = out_block(4 * zm + 2 * du + 1).astype(BF)
            r.G["O"][k : k + 48, :] = out_block(4 * zm + 2 * du)
        rs1_send("O", zm)

    wait_recv("gas", r.GA.at[:, oth_rows, :])
    for n in ("DQ", "DK", "DV"):
        for i in range(3):
            getattr(r, n)[i] = jnp.zeros((512, 128), BF)

    def s1(p, zm):
        return functools.partial(rs_sum1, p, zm)

    def s2a(p, zm):
        return functools.partial(rs_sum2a, p, zm)

    def s2c(p):
        return functools.partial(rs_sum2c, p)

    def vs(s):
        return functools.partial(vec_step, 1, s)

    bw_hooks = [
        [s1("U", 1), s2a("D", 3), s2a("D", 2), vs(0)],
        [s1("U", 0), s2a("D", 1), s2a("D", 0), s2c("D")],
        [s2a("U", 3), s2a("U", 2), vs(1), s1("O", 3), s1("O", 2)],
        [s2a("U", 1), s2a("U", 0), s2c("U"), s1("O", 1), s1("O", 0)],
        [functools.partial(rs_final, "D"), vs(2)],
        [s2a("O", 3), s2a("O", 2), s2a("O", 1), s2a("O", 0), s2c("O"), vs(3)],
    ]

    def bwd_head(h, carry):
        at_index(h, bw_hooks)
        i = lax.div(h, 2)
        a = lax.rem(h, 2)
        go = half(r.GA[i], a)
        for t in range(4):
            q = slice(128 * t, 128 * t + 128)
            prob = r.P32[h, q, :]
            dp = mm(go[q], r.V3[i], 1, 1)
            delta = jnp.sum(prob * dp, axis=1, keepdims=True)
            r.DSB[q, :] = (prob * (dp - delta)).astype(BF)
            r.PB[q, :] = prob.astype(BF)
        r.DV[i] = r.DV[i] + mm(r.PB[...], go, 0, 0).astype(BF)
        dq = mm(r.DSB[...], half(r.K3[i], a)) * 0.125
        r.DQ[i] = r.DQ[i] + dq.astype(BF)
        dk = mm(r.DSB[...], half(r.Q3[i], a), 0, 0)
        r.DK[i] = r.DK[i] + dk.astype(BF)
        return carry

    lax.fori_loop(0, 6, bwd_head, 0)

    all512 = pl.ds(0, 512)
    for k, n in enumerate(("DQ", "DK", "DV")):
        r.T[:, 384 * k : 384 * k + 384] = mm(r.X[...], joined(getattr(r, n), all512), 0, 0)
    for zm in (3, 2, 1, 0):
        stage("Q", zm, r.T, 192 * zs[zm])
    run([functools.partial(rs_final, "U"), vs(4)])

    for rows in (oth_rows, own_rows):
        acc = mm(joined(r.DQ, rows), r.WQ[:, 0:384], 1, 1)
        acc = acc + mm(joined(r.DK, rows), r.WQ[:, 384:768], 1, 1)
        acc = acc + mm(joined(r.DV, rows), r.WQ[:, 768:1152], 1, 1)
        if rows is oth_rows:
            r.IGS[...] = acc.astype(BF)
            send("ig", r.IGS, r.IGR, partner)
        else:
            r.GS[...] = r.GS[...] + acc
    wait_recv("ig", r.IGR)
    r.ig[...] = (r.GS[...] + r.IGR[...].astype(F32)).astype(BF)

    for zm in (3, 2, 1, 0):
        rs_sum1("Q", zm)
    rs_final("O")
    for zm in (3, 2, 1, 0):
        rs_sum2a("Q", zm)
    rs_sum2c("Q")
    r.dwd[...] = r.G["D"][0:96, :]
    r.UT[0:96, :] = r.G["U"][0:96, :]
    r.UT[96:128, :] = jnp.zeros((32, 768), F32)
    r.dwu[...] = jnp.transpose(r.UT[...])[:, 0:96]
    go = r.G["O"][0:48, :]
    r.dwo[...] = jnp.concatenate([go[0:24], go[24:48]], axis=1)
    back = pltpu.roll(r.VS[88:96, :], lax.rem(768 - 24 * flat, 768), 1)
    for k, n in enumerate(("dga", "dba", "dgf", "dbf")):
        getattr(r, n)[...] = back[k, 0:24]
    rs_final("Q")
    r.dwq[...] = r.G["Q"][0:48, 0:384]
    r.dwk[...] = r.G["Q"][0:48, 384:768]
    r.dwv[...] = r.G["Q"][0:48, 768:1152]

    for entry in sends:
        if entry[3] not in waited:
            wait_send(entry)


def layer_small(*args):
    shapes = (
        ((256, 768), BF),
        ((256, 768), BF),
        ((48, 384), F32),
        ((48, 384), F32),
        ((48, 384), F32),
        ((24, 768), F32),
        ((24,), F32),
        ((24,), F32),
        ((768, 96), F32),
        ((96, 768), F32),
        ((24,), F32),
        ((24,), F32),
    )
    vmem = pl.BlockSpec(memory_space=pltpu.VMEM)
    smem = pl.BlockSpec(memory_space=pltpu.SMEM)
    return pl.pallas_call(
        layer_kernel,
        out_shape=tuple(jax.ShapeDtypeStruct(s, d) for s, d in shapes),
        in_specs=[smem if n in ("len", "off") else vmem for n in IN_NAMES],
        out_specs=tuple(vmem for _ in shapes),
        scratch_shapes=[s for _, s in scratch_list()],
        compiler_params=pltpu.CompilerParams(
            collective_id=0, has_side_effects=True, vmem_limit_bytes=67043328
        ),
    )(*args)


def labels_of(lengths, offsets):
    position = jnp.arange(BIN, dtype=jnp.int32)[:, None]
    starts = offsets[None, :]
    inside = (position >= starts) & (position < starts + lengths[None, :])
    slot_order = jnp.arange(1, lengths.shape[0] + 1, dtype=jnp.int32)[None, :]
    return jnp.sum(jnp.where(inside, slot_order, 0), axis=1)


def layer_norm(operand, gain_vec, bias_vec):
    row_mean = jnp.mean(operand, axis=-1, keepdims=True)
    centered = operand - row_mean
    inverse = lax.rsqrt(jnp.mean(centered * centered, axis=-1, keepdims=True) + EPS)
    normed = centered * inverse
    return (normed * gain_vec + bias_vec, normed, inverse)


def norm_back(grad_rows, normed, inverse, gain_vec):
    scaled = grad_rows * gain_vec
    inner = jnp.mean(scaled * normed, axis=-1, keepdims=True)
    return inverse * (scaled - jnp.mean(scaled, axis=-1, keepdims=True) - normed * inner)


def gelu_exact(operand):
    return jax.nn.gelu(operand, approximate=False)


def contract_rows(left, right):
    return lax.dot_general(
        left, right, (((0,), (0,)), ((), ())), preferred_element_type=F32
    )


def contract_cols(left, right):
    return lax.dot_general(
        left, right, (((1,), (1,)), ((), ())), preferred_element_type=F32
    )


def score_block(queries, key_rows, labels_bin, factor):
    scores = (
        jnp.einsum("qhd,khd->hqk", queries, key_rows, preferred_element_type=F32) * factor
    )
    allowed = ((labels_bin[:, None] == labels_bin[None, :]) & (labels_bin[:, None] > 0))[None]
    live_rows = (labels_bin > 0)[None, :, None]
    return (scores, allowed, live_rows)


def masked_exp(scores, allowed, row_top):
    return jnp.where(allowed, jnp.exp(jnp.where(allowed, scores - row_top, 0.0)), 0.0)


def attend_bin(pieces, factor):
    queries, key_rows, value_rows, labels_bin = pieces
    scores, allowed, live_rows = score_block(queries, key_rows, labels_bin, factor)
    row_top = jnp.max(jnp.where(allowed, scores, -1e30), axis=2, keepdims=True)
    row_top = jnp.where(live_rows, row_top, 0.0)
    weights = masked_exp(scores, allowed, row_top)
    denominator = jnp.sum(weights, axis=2, keepdims=True) + jnp.where(live_rows, 0.0, 1.0)
    probability = (weights / denominator).astype(jnp.bfloat16)
    mixed_rows = jnp.einsum(
        "hqk,khd->qhd", probability, value_rows, preferred_element_type=F32
    )
    return (mixed_rows.astype(jnp.bfloat16), row_top, denominator)


def attend_back(pieces, factor):
    queries, key_rows, value_rows, labels_bin, row_top, denominator, grad_mixed = pieces
    scores, allowed, live_rows = score_block(queries, key_rows, labels_bin, factor)
    probability = masked_exp(scores, allowed, row_top) / denominator
    grad_values = jnp.einsum(
        "hqk,qhd->khd",
        probability.astype(jnp.bfloat16),
        grad_mixed,
        preferred_element_type=F32,
    )
    grad_probs = jnp.einsum(
        "qhd,khd->hqk", grad_mixed, value_rows, preferred_element_type=F32
    )
    row_delta = jnp.sum(probability * grad_probs, axis=2, keepdims=True)
    grad_scores = (probability * (grad_probs - row_delta)).astype(jnp.bfloat16)
    grad_queries = (
        jnp.einsum("hqk,khd->qhd", grad_scores, key_rows, preferred_element_type=F32)
        * factor
    )
    grad_keys = (
        jnp.einsum("hqk,qhd->khd", grad_scores, queries, preferred_element_type=F32)
        * factor
    )
    return (
        grad_queries.astype(jnp.bfloat16),
        grad_keys.astype(jnp.bfloat16),
        grad_values.astype(jnp.bfloat16),
    )


def per_device(
    tokens,
    w_query,
    w_key,
    w_value,
    w_out,
    gain_attn,
    bias_attn,
    w_up,
    w_down,
    gain_ffn,
    bias_ffn,
    seq_lengths,
    seq_offsets,
    out_grad,
):
    low_type = jnp.bfloat16
    bin_count = seq_lengths.shape[0]
    group_rows = bin_count * BIN
    head_width = w_query.shape[1]
    local_heads = head_width // HD
    factor = 1.0 / math.sqrt(HD)
    labels = jax.vmap(labels_of)(seq_lengths, seq_offsets)
    full_query, full_key, full_value = (
        lax.all_gather(w_query.astype(low_type), DP, axis=0, tiled=True),
        lax.all_gather(w_key.astype(low_type), DP, axis=0, tiled=True),
        lax.all_gather(w_value.astype(low_type), DP, axis=0, tiled=True),
    )
    projection = jnp.concatenate([full_query, full_key, full_value], axis=1)
    whole_rows = lax.all_gather(tokens, HEAD, axis=0, tiled=True)
    projected = jnp.dot(whole_rows, projection, preferred_element_type=F32).astype(low_type)
    shape_bins = (bin_count, BIN, local_heads, HD)
    queries = projected[:, :head_width].reshape(shape_bins)
    key_rows = projected[:, head_width : 2 * head_width].reshape(shape_bins)
    value_rows = projected[:, 2 * head_width :].reshape(shape_bins)
    mixed_bins, row_tops, denominators = lax.map(
        lambda pieces: attend_bin(pieces, factor), (queries, key_rows, value_rows, labels)
    )
    attended = mixed_bins.reshape(group_rows, head_width)
    out_full, up_part, down_part, gain_one, bias_one, gain_two, bias_two = (
        lax.all_gather(w_out.astype(low_type), BOTH, axis=0, tiled=True),
        lax.all_gather(w_up.astype(low_type), BOTH, axis=1, tiled=True),
        lax.all_gather(w_down.astype(low_type), BOTH, axis=0, tiled=True),
        lax.all_gather(gain_attn.astype(low_type), BOTH, axis=0, tiled=True),
        lax.all_gather(bias_attn.astype(low_type), BOTH, axis=0, tiled=True),
        lax.all_gather(gain_ffn.astype(low_type), BOTH, axis=0, tiled=True),
        lax.all_gather(bias_ffn.astype(low_type), BOTH, axis=0, tiled=True),
    )
    gain_first = gain_one.astype(F32)
    gain_second = gain_two.astype(F32)
    token_view = lax.all_to_all(attended, HEAD, split_axis=0, concat_axis=1, tiled=True)
    first_sum = tokens.astype(F32) + jnp.dot(
        token_view, out_full, preferred_element_type=F32
    )
    normed_one, unit_one, inverse_one = layer_norm(
        first_sum, gain_first, bias_one.astype(F32)
    )
    ffn_input = normed_one.astype(low_type)
    pre_act = jnp.dot(ffn_input, up_part, preferred_element_type=F32)
    activated, gelu_pull = jax.vjp(gelu_exact, pre_act)
    hidden = activated.astype(low_type)
    second_sum = normed_one + jnp.dot(hidden, down_part, preferred_element_type=F32)
    result, unit_two, inverse_two = layer_norm(
        second_sum, gain_second, bias_two.astype(F32)
    )
    output = result.astype(low_type)
    grad_result = out_grad.astype(F32)
    grad_gain_two = jnp.sum(grad_result * unit_two, axis=0)
    grad_bias_two = jnp.sum(grad_result, axis=0)
    grad_second = norm_back(grad_result, unit_two, inverse_two, gain_second)
    grad_ffn = grad_second.astype(low_type)
    grad_down_part = contract_rows(hidden, grad_ffn)
    grad_pre = gelu_pull(contract_cols(grad_ffn, down_part))[0].astype(low_type)
    grad_up_part = contract_rows(ffn_input, grad_pre)
    grad_normed = grad_second + contract_cols(grad_pre, up_part)
    grad_gain_one = jnp.sum(grad_normed * unit_one, axis=0)
    grad_bias_one = jnp.sum(grad_normed, axis=0)
    grad_first = norm_back(grad_normed, unit_one, inverse_one, gain_first)
    grad_branch = grad_first.astype(low_type)
    grad_out_full = contract_rows(token_view, grad_branch)
    part_out, part_up, part_down, part_gain_one, part_bias_one, part_gain_two, part_bias_two = (
        lax.psum_scatter(grad_out_full, BOTH, scatter_dimension=0, tiled=True),
        lax.psum_scatter(grad_up_part, BOTH, scatter_dimension=1, tiled=True),
        lax.psum_scatter(grad_down_part, BOTH, scatter_dimension=0, tiled=True),
        lax.psum_scatter(grad_gain_one, BOTH, scatter_dimension=0, tiled=True),
        lax.psum_scatter(grad_bias_one, BOTH, scatter_dimension=0, tiled=True),
        lax.psum_scatter(grad_gain_two, BOTH, scatter_dimension=0, tiled=True),
        lax.psum_scatter(grad_bias_two, BOTH, scatter_dimension=0, tiled=True),
    )
    grad_token_view = contract_cols(grad_branch, out_full).astype(low_type)
    grad_attended = lax.all_to_all(grad_token_view, HEAD, split_axis=1, concat_axis=0, tiled=True)
    grad_bins = grad_attended.reshape(shape_bins)
    grad_queries, grad_keys, grad_values = lax.map(
        lambda pieces: attend_back(pieces, factor),
        (queries, key_rows, value_rows, labels, row_tops, denominators, grad_bins),
    )
    grad_projected = jnp.concatenate(
        [
            grad_queries.reshape(group_rows, head_width),
            grad_keys.reshape(group_rows, head_width),
            grad_values.reshape(group_rows, head_width),
        ],
        axis=1,
    )
    grad_projection = contract_rows(whole_rows, grad_projected)
    part_query, part_key, part_value = (
        lax.psum_scatter(grad_projection[:, :head_width], DP, scatter_dimension=0, tiled=True),
        lax.psum_scatter(
            grad_projection[:, head_width : 2 * head_width], DP, scatter_dimension=0, tiled=True
        ),
        lax.psum_scatter(
            grad_projection[:, 2 * head_width :], DP, scatter_dimension=0, tiled=True
        ),
    )
    input_grad = (
        grad_first
        + lax.psum_scatter(
            contract_cols(grad_projected, projection).astype(jnp.bfloat16),
            HEAD,
            scatter_dimension=0,
            tiled=True,
        ).astype(F32)
    ).astype(low_type)
    return (
        output,
        input_grad,
        part_query,
        part_key,
        part_value,
        part_out,
        part_gain_one,
        part_bias_one,
        part_up,
        part_down,
        part_gain_two,
        part_bias_two,
    )


def solution(mesh):
    small = mesh.shape[DP] == 16 and mesh.shape[HEAD] == 2
    return jax.shard_map(
        layer_small if small else per_device,
        mesh=mesh,
        in_specs=(
            P(BOTH, None),
            P(DP, HEAD),
            P(DP, HEAD),
            P(DP, HEAD),
            P(BOTH, None),
            P(BOTH),
            P(BOTH),
            P(None, BOTH),
            P(BOTH, None),
            P(BOTH),
            P(BOTH),
            P(DP, None),
            P(DP, None),
            P(BOTH, None),
        ),
        out_specs=(
            P(BOTH, None),
            P(BOTH, None),
            P(DP, HEAD),
            P(DP, HEAD),
            P(DP, HEAD),
            P(BOTH, None),
            P(BOTH),
            P(BOTH),
            P(None, BOTH),
            P(BOTH, None),
            P(BOTH),
            P(BOTH),
        ),
        check_vma=False,
    )
```

time: 1050 us -> 185 us (0.18)
  waiting for transfers between devices: 712 us -> 0 us
  blocking collectives: 218 us -> 0 us
  Pallas kernels: 0 us -> 172 us
  matrix products: 57.8 us -> 0 us
  other arithmetic: 17.9 us -> 0 us
  between operations: 15 us -> 0.68 us
    reduce_scatter x4 -> x0, waiting for transfers between devices: 388 us -> none  [the longest x1 142 us: per_device(): lax.psum_scatter(grad_up_part, ('dp', 'head'), scatter_dimension=1, tiled...]
    unnamed x13 -> x0, waiting for transfers between devices: 325 us -> none
    pallas_call x0 -> x1, Pallas kernels: none -> 172 us  [layer_small(): pl.pallas_call(layer_kernel, out_shape=tuple((jax.ShapeDtypeStruct(s, d)...]
    all_gather x4 -> x0, blocking collectives: 133 us -> none  [the longest x1 46 us: per_device(): lax.all_gather(w_query.astype(low_type), 'dp', axis=0, tiled=True)]
    unnamed x2 -> x0, blocking collectives: 79.9 us -> none
    dot_general x18 -> x0, matrix products: 57.8 us -> none  [the longest x4 17.3 us: contract_rows(): lax.dot_general(left, right, (((0,), (0,)), ((), ())), preferred_element_...]
    convert_element_type x16 -> x0, other arithmetic: 11.5 us -> none  [the longest x1 2.15 us: attend_back(): grad_scores = (probability * (grad_probs - row_delta)).astype(jnp.bfloat16)]
  transfers between devices with their start and end apart: 11 -> 0, of which waited for: 6 -> 0; matrix products, arithmetic and copies ran while one was open for 6% -> 0% of each run, Pallas kernels for 0% -> 0%
where the time goes in v1:
time: 185 us
  Pallas kernels  172 us (93%)
  local copies, waits for them, and re-layouts  11.6 us (6%)
    pallas_call x1, Pallas kernels, layer_small(): pl.pallas_call(layer_kernel, out_shape=tuple((jax.ShapeDtypeStruct(s, d)...  172 us
    unnamed x34, local copies, waits for them, and re-layouts  9.73 us

profile of v1, /device:TPU:0, one launch (start us, length us, event | category | flops | bytes accessed | tf_op | source)
XLA Modules:
  0.0 184.6 jit_solution(7455106848753866954)
XLA Ops:
  0.6 1.9 %copy.26.refs_7_ = f32[768,96]{1,0:T(8,128)} copy(f32[768,96]{0,1:T(8,128)} %param.21) | data formatting | bytes 589824 | tf_op args[7]
  2.5 172.3 %shard_map.229 = (bf16[256,768]{1,0:T(8,128)(2,1)}, bf16[256,768]{1,0:T(8,128)(2,1)}, f32[48,384]{1,0:T(8,128)}, f32[48,384]{1,0:T(8,128)}, f32[48,384]{1,0:T(8,...) custom-call(bf16[256,768]{1,0:T(8,128)(2,1)} %refs_0_.1, ...), custom_call_target="tpu_custom_call" | custom-call | tf_op jit(solution)/shard_map/pallas_call | solution.py:741
  174.8 0.0 copy-start.1
  174.8 1.9 %copy.27 = f32[768,96]{0,1:T(8,128)} copy(f32[768,96]{1,0:T(8,128)} %get-tuple-element.20) | data formatting | bytes 589824 | tf_op jit(solution)/shard_map/pallas_call | solution.py:741
  176.7 0.0 copy-done.1
  176.7 0.0 copy-start
  176.7 0.7 copy.39
  177.5 0.4 copy-done
  177.9 0.0 copy-start.6
  177.9 0.0 copy-start.5
  177.9 0.0 copy-start.4
  177.9 0.7 copy.40
  178.6 0.2 copy-done.6
  178.8 0.0 copy-start.2
  178.8 0.6 copy.41
  179.4 0.0 copy-done.5
  179.4 0.6 copy.42
  180.1 0.0 copy-done.4
  180.1 0.0 copy-start.3
  180.1 0.6 copy.43
  180.7 0.3 copy-done.3
  181.0 0.0 copy-start.10
  181.0 0.6 copy.44
  181.6 0.0 copy-done.10
  181.6 0.0 copy-start.9
  181.6 0.5 copy.45
  182.1 0.2 copy-done.9
  182.3 0.5 copy.46
  182.8 0.0 copy-done.2
  182.8 0.0 copy-start.8
  182.8 0.7 copy.47
  183.5 0.0 copy-done.8
  183.5 0.0 copy-start.7
  183.5 0.5 copy.48
  184.0 0.1 copy-done.7
  184.1 0.5 copy.49
Async XLA Ops:
  174.8 1.9 %copy-start.1 = (bf16[256,768]{1,0:T(8,128)(2,1)S(1)}, bf16[256,768]{1,0:T(8,128)(2,1)}, u32[]{:S(2)}) copy-start(bf16[256,768]{1,0:T(8,128)(2,1)} %get-tuple-element.36) | copy-start | bytes 1179652
  176.7 1.1 copy-start
  177.9 0.9 copy-start.6
  177.9 1.5 copy-start.5
  177.9 2.2 %copy-start.4 = (f32[48,384]{1,0:T(8,128)S(1)}, f32[48,384]{1,0:T(8,128)}, u32[]{:S(2)}) copy-start(f32[48,384]{1,0:T(8,128)} %get-tuple-element.40) | copy-start | bytes 221188
  178.8 4.0 %copy-start.2 = (f32[96,768]{1,0:T(8,128)S(1)}, f32[96,768]{1,0:T(8,128)}, u32[]{:S(2)}) copy-start(f32[96,768]{1,0:T(8,128)} %get-tuple-element.45) | copy-start | bytes 884740
  180.1 0.9 copy-start.3
  181.0 0.6 copy-start.10
  181.6 0.7 copy-start.9
  182.8 0.7 copy-start.8
  183.5 0.6 copy-start.7

commit v2 on v1

--- a/solution.py
+++ b/solution.py
@@ -75,7 +75,6 @@
             add(key + p, (size, c), F32 if key == "G" else BF)
     add("VS", (96, 768), F32)
     add("VR", (80, 768), F32)
-    add("UT", (128, 768), F32)
     items.append(("ss", pltpu.SemaphoreType.DMA((320,))))
     items.append(("rs", pltpu.SemaphoreType.DMA((320,))))
     items.append(("ls", pltpu.SemaphoreType.DMA((4,))))
@@ -355,8 +354,7 @@
         [wo[:, 0:384], wo[:, 384:768]], axis=0
     ).astype(BF)
     ag_own("O")
-    wut = jnp.transpose(jnp.concatenate([r.wu[...], jnp.zeros((768, 32), F32)], axis=1))
-    r.WU[pl.ds(pl.multiple_of(me * 96, 16), 96), :] = wut[0:96, :].astype(BF)
+    r.WU[pl.ds(pl.multiple_of(me * 96, 16), 96), :] = r.wu[...].astype(BF)
     r.WD[pl.ds(pl.multiple_of(me * 96, 16), 96), :] = r.wd[...].astype(BF)
 
     col_pos = lax.broadcasted_iota(jnp.int32, (512, 128), 0)
@@ -703,9 +701,7 @@
         rs_sum2a("Q", zm)
     rs_sum2c("Q")
     r.dwd[...] = r.G["D"][0:96, :]
-    r.UT[0:96, :] = r.G["U"][0:96, :]
-    r.UT[96:128, :] = jnp.zeros((32, 768), F32)
-    r.dwu[...] = jnp.transpose(r.UT[...])[:, 0:96]
+    r.dwu[...] = r.G["U"][0:96, :]
     go = r.G["O"][0:48, :]
     r.dwo[...] = jnp.concatenate([go[0:24], go[24:48]], axis=1)
     back = pltpu.roll(r.VS[88:96, :], lax.rem(768 - 24 * flat, 768), 1)
@@ -719,6 +715,12 @@
     for entry in sends:
         if entry[3] not in waited:
             wait_send(entry)
+
+
+def hand_over(*refs):
+    half = len(refs) // 2
+    for src, dst in zip(refs[:half], refs[half:]):
+        dst[...] = src[...]
 
 
 def layer_small(*args):
@@ -731,16 +733,19 @@
         ((24, 768), F32),
         ((24,), F32),
         ((24,), F32),
-        ((768, 96), F32),
+        ((96, 768), F32),
         ((96, 768), F32),
         ((24,), F32),
         ((24,), F32),
     )
     vmem = pl.BlockSpec(memory_space=pltpu.VMEM)
     smem = pl.BlockSpec(memory_space=pltpu.SMEM)
-    return pl.pallas_call(
+    out_shape = tuple(jax.ShapeDtypeStruct(s, d) for s, d in shapes)
+    up = IN_NAMES.index("wu")
+    args = args[:up] + (args[up].T,) + args[up + 1 :]
+    outs = pl.pallas_call(
         layer_kernel,
-        out_shape=tuple(jax.ShapeDtypeStruct(s, d) for s, d in shapes),
+        out_shape=out_shape,
         in_specs=[smem if n in ("len", "off") else vmem for n in IN_NAMES],
         out_specs=tuple(vmem for _ in shapes),
         scratch_shapes=[s for _, s in scratch_list()],
@@ -748,6 +753,14 @@
             collective_id=0, has_side_effects=True, vmem_limit_bytes=67043328
         ),
     )(*args)
+    outs = pl.pallas_call(
+        hand_over,
+        out_shape=out_shape,
+        in_specs=[vmem for _ in shapes],
+        out_specs=tuple(vmem for _ in shapes),
+    )(*outs)
+    up = OUT_NAMES.index("dwu")
+    return outs[:up] + (outs[up].T,) + outs[up + 1 :]
 
 
 def labels_of(lengths, offsets):

time: 185 us -> 176 us (0.951)
  local copies, waits for them, and re-layouts: 11.6 us -> 0 us
  Pallas kernels: 172 us -> 175 us
    unnamed x34 -> x0, local copies, waits for them, and re-layouts: 9.73 us -> none
    pallas_call x1 -> x2, Pallas kernels: 172 us -> 175 us  [the longest x1 172 us: layer_small(): pl.pallas_call(layer_kernel, out_shape=out_shape, in_specs=[smem if n in...]
    pallas_call x1 -> x0, local copies, waits for them, and re-layouts: 1.92 us -> none  [layer_small(): pl.pallas_call(layer_kernel, out_shape=tuple((jax.ShapeDtypeStruct(s, d)...]
where the time goes in v2:
time: 176 us
  Pallas kernels  175 us (99%)
    pallas_call x1, Pallas kernels, layer_small(): pl.pallas_call(layer_kernel, out_shape=out_shape, in_specs=[smem if n in...  172 us

profile of v2, /device:TPU:0, one launch (start us, length us, event | category | flops | bytes accessed | tf_op | source)
XLA Modules:
  0.0 175.8 jit_solution(5993351070210973435)
XLA Ops:
  0.6 172.3 %shard_map.229 = (bf16[256,768]{1,0:T(8,128)(2,1)}, bf16[256,768]{1,0:T(8,128)(2,1)}, f32[48,384]{1,0:T(8,128)}, f32[48,384]{1,0:T(8,128)}, f32[48,384]{1,0:T(8,...) custom-call(bf16[256,768]{1,0:T(8,128)(2,1)} %refs_0_.1, ...), custom_call_target="tpu_custom_call" | custom-call | tf_op jit(solution)/shard_map/pallas_call | solution.py:746
  173.0 2.6 %shard_map.230 = (bf16[256,768]{1,0:T(8,128)(2,1)}, bf16[256,768]{1,0:T(8,128)(2,1)}, f32[48,384]{1,0:T(8,128)}, f32[48,384]{1,0:T(8,128)}, f32[48,384]{1,0:T(8,...) custom-call(bf16[256,768]{1,0:T(8,128)(2,1)} %get-tuple-element.36.r, ...), custom_call_target="tpu_custom_call" | custom-call | tf_op jit(solution)/shard_map/pallas_call | solution.py:756

commit v3 on v2

--- a/solution.py
+++ b/solution.py
@@ -24,6 +24,7 @@
 PER_PIECE = ("G", "S1", "R1", "S2A", "R2A", "S3A", "R3A", "S2C", "R2C", "S3C", "R3C")
 DP, HEAD = "dp", "head"
 BOTH = (DP, HEAD)
+COPIES = 200
 
 
 def mm(a, b, ca=1, cb=0):
@@ -75,9 +76,9 @@
             add(key + p, (size, c), F32 if key == "G" else BF)
     add("VS", (96, 768), F32)
     add("VR", (80, 768), F32)
-    items.append(("ss", pltpu.SemaphoreType.DMA((320,))))
-    items.append(("rs", pltpu.SemaphoreType.DMA((320,))))
-    items.append(("ls", pltpu.SemaphoreType.DMA((4,))))
+    items.append(("ss", pltpu.SemaphoreType.DMA((COPIES,))))
+    items.append(("rs", pltpu.SemaphoreType.DMA((COPIES,))))
+    items.append(("ls", pltpu.SemaphoreType.DMA((1,))))
     return items
 
 
@@ -194,9 +195,9 @@
         wait_recv(("ag", p, part, m), wslice(p, part, m))
 
     def ag_own(p):
+        forward(p, "C", 0, MU)
         for f in (4, 8, 12):
             forward(p, "A", 0, f)
-        forward(p, "C", 0, MU)
         forward(p, "A", 0, MU)
         forward(p, "A", 0, MV)
         for f in (4, 8, 12):
@@ -234,10 +235,13 @@
         for s in steps:
             s()
 
-    vec_peer = (partner, (ids[MU], c), (ids[MV], c), (ids[4], c), (ids[8], c))
+    vec_peers = (
+        (partner, (ids[MU], c), (ids[MV], c), (ids[4], c), (ids[8], c)),
+        (partner, (ids[4], c), (ids[8], c), (ids[MU], c), (ids[MV], c)),
+    )
 
     def vec_send(k, s):
-        send(("v", k, s), r.VS.at[pl.ds(48 * k + 8 * s, 8), :], r.VR.at[pl.ds(40 * k + 8 * s, 8), :], vec_peer[s])
+        send(("v", k, s), r.VS.at[pl.ds(48 * k + 8 * s, 8), :], r.VR.at[pl.ds(40 * k + 8 * s, 8), :], vec_peers[k][s])
 
     def vec_step(k, s):
         src, got_row = pl.ds(48 * k + 8 * s, 8), pl.ds(40 * k + 8 * s, 8)
@@ -374,14 +378,15 @@
         same = lab == jnp.broadcast_to(row_lab[0:1], (128, 512))
         r.BIAS[q, :] = jnp.where(same, 0.0, -1e30).astype(F32)
 
-    run(ag_steps("Q")[:7])
+    q_steps, o_steps, u_steps, d_steps = (ag_steps(p) for p in PIECES)
+    run(q_steps[:5])
     ag_own("U")
-    run(ag_steps("Q")[7:])
-    o_steps, u_steps, d_steps = ag_steps("O"), ag_steps("U"), ag_steps("D")
     vec_step(0, 0)
+    run(o_steps[:5])
+    run(q_steps[5:])
+    ag_own("D")
     wait_recv("tok", r.X.at[own_rows, :])
     local.wait()
-    run(o_steps[:4])
     for zm in range(4):
         ag_plane("Q", zm)
 
@@ -392,18 +397,18 @@
             full = full * BF(0.125)
         for i in range(3):
             getattr(r, n)[i] = full[:, 128 * i : 128 * i + 128]
-    ag_own("D")
     vec_step(0, 1)
+    run(u_steps[:2])
 
     for i in range(3):
         r.ATT[i] = jnp.zeros((512, 128), BF)
     fw_hooks = [
-        o_steps[4:9],
-        o_steps[9:] + u_steps[:1],
-        [functools.partial(vec_step, 0, 2)] + u_steps[1:4],
-        u_steps[4:7],
-        [functools.partial(vec_step, 0, 3)] + u_steps[7:10],
-        u_steps[10:],
+        u_steps[2:5],
+        [functools.partial(vec_step, 0, 2)] + o_steps[5:8],
+        o_steps[8:12],
+        o_steps[12:] + d_steps[:1] + [functools.partial(vec_step, 0, 3)],
+        d_steps[1:3],
+        d_steps[3:5],
     ]
     lane = lax.broadcasted_iota(jnp.int32, (1, 128), 1)
 
@@ -444,7 +449,7 @@
     for zm in range(4):
         ag_plane("O", zm)
     send("wop", r.WOP.at[c], r.WOP.at[c], partner)
-    run(d_steps[:4])
+    run(u_steps[5:8])
     vec_step(0, 4)
     wait_recv("wop", r.WOP.at[1 - c])
 
@@ -468,7 +473,7 @@
     branch = mm(joined(r.ATT, own_rows), r.WO[own_heads, :])
     branch = branch + mm(joined(r.ATTR, all256), r.WO[oth_heads, :])
     r.GS[...] = branch
-    run(d_steps[4:6])
+    run(u_steps[8:11])
 
     def norm(val):
         mean = jnp.mean(val, axis=1, keepdims=True)
@@ -488,7 +493,7 @@
 
     lax.fori_loop(0, 4, ln1, 0)
     send("fin", r.FIN.at[own_rows, :], r.FIN.at[own_rows, :], partner)
-    run(d_steps[6:8])
+    run(u_steps[11:])
     wait_recv("fin", r.FIN.at[oth_rows, :])
 
     def plane_rows(zm):
@@ -511,7 +516,7 @@
 
         lax.fori_loop(0, 8, act, 0)
 
-    d_groups = (d_steps[8:10], d_steps[10:12], d_steps[12:], [])
+    d_groups = (d_steps[5:8], d_steps[8:11], d_steps[11:], [])
     for zm in range(4):
         ag_plane("U", zm)
         ffn_up(zm)
@@ -566,8 +571,9 @@
             r.SEC[rows, :] = part
             if n_done == 3 and rows is oth_rows:
                 send("gn", r.SEC.at[oth_rows, :], r.SECR, partner)
-        if n_done:
-            rs_sum1("D", zm + 1)
+        if n_done == 2:
+            rs_sum1("D", 3)
+    rs_sum1("U", 3)
     wait_recv("gn", r.SECR)
 
     def ln1_back(t, sums):
@@ -599,7 +605,8 @@
     gview = mm(r.GB[...], r.WO[own_heads, :], 1, 1).astype(BF)
     for i in range(3):
         r.GA[i, own_rows, :] = gview[:, 128 * i : 128 * i + 128]
-    rs_sum1("D", 0)
+    vec_step(1, 0)
+    rs_sum1("D", 2)
     r.T[own_heads, 0:768] = mm(joined(r.ATT, own_rows), r.GB[...], 0, 0)
     r.T[oth_heads, 0:768] = mm(joined(r.ATTR, all256), r.GB[...], 0, 0)
 
@@ -611,8 +618,7 @@
 
     lax.fori_loop(0, 16, pair_out, 0)
     send("s0", r.S0, r.R0, partner)
-    rs_sum1("U", 3)
-    rs_sum1("U", 2)
+    rs_sum2a("D", 3)
     wait_recv("s0", r.R0)
 
     def out_block(m):
@@ -646,12 +652,12 @@
         return functools.partial(vec_step, 1, s)
 
     bw_hooks = [
-        [s1("U", 1), s2a("D", 3), s2a("D", 2), vs(0)],
-        [s1("U", 0), s2a("D", 1), s2a("D", 0), s2c("D")],
-        [s2a("U", 3), s2a("U", 2), vs(1), s1("O", 3), s1("O", 2)],
-        [s2a("U", 1), s2a("U", 0), s2c("U"), s1("O", 1), s1("O", 0)],
-        [functools.partial(rs_final, "D"), vs(2)],
-        [s2a("O", 3), s2a("O", 2), s2a("O", 1), s2a("O", 0), s2c("O"), vs(3)],
+        [s2a("U", 3), vs(1)],
+        [s1("U", 2)],
+        [s2a("D", 2), vs(2)],
+        [s1("D", 1)],
+        [s2a("U", 2), vs(3)],
+        [],
     ]
 
     def bwd_head(h, carry):
@@ -680,7 +686,7 @@
         r.T[:, 384 * k : 384 * k + 384] = mm(r.X[...], joined(getattr(r, n), all512), 0, 0)
     for zm in (3, 2, 1, 0):
         stage("Q", zm, r.T, 192 * zs[zm])
-    run([functools.partial(rs_final, "U"), vs(4)])
+    run([s1("U", 1), s2a("D", 1)])
 
     for rows in (oth_rows, own_rows):
         acc = mm(joined(r.DQ, rows), r.WQ[:, 0:384], 1, 1)
@@ -689,17 +695,19 @@
         if rows is oth_rows:
             r.IGS[...] = acc.astype(BF)
             send("ig", r.IGS, r.IGR, partner)
+            run([s1("D", 0), s2a("U", 1)])
         else:
             r.GS[...] = r.GS[...] + acc
     wait_recv("ig", r.IGR)
     r.ig[...] = (r.GS[...] + r.IGR[...].astype(F32)).astype(BF)
 
-    for zm in (3, 2, 1, 0):
-        rs_sum1("Q", zm)
-    rs_final("O")
-    for zm in (3, 2, 1, 0):
-        rs_sum2a("Q", zm)
-    rs_sum2c("Q")
+    run([s1("U", 0), s2a("D", 0), s2c("D"), s2a("U", 0), s2c("U")])
+    run([s1("O", 3), s1("O", 2), s2a("O", 3), s1("O", 1), s2a("O", 2), s1("O", 0)])
+    run([s2a("O", 1), s2a("O", 0), vs(4), s2c("O")])
+    run([s1("Q", 3), s1("Q", 2), s2a("Q", 3), s1("Q", 1), s2a("Q", 2), s1("Q", 0)])
+    run([s2a("Q", 1), s2a("Q", 0), s2c("Q")])
+    for p in ("D", "U", "O"):
+        rs_final(p)
     r.dwd[...] = r.G["D"][0:96, :]
     r.dwu[...] = r.G["U"][0:96, :]
     go = r.G["O"][0:48, :]

time: 176 us -> 159 us (0.903)
  Pallas kernels: 175 us -> 158 us
    pallas_call x1, Pallas kernels: 172 us -> 156 us  [layer_small(): pl.pallas_call(layer_kernel, out_shape=out_shape, in_specs=[smem if n in...]
where the time goes in v3:
time: 159 us
  Pallas kernels  158 us (99%)
    pallas_call x1, Pallas kernels, layer_small(): pl.pallas_call(layer_kernel, out_shape=out_shape, in_specs=[smem if n in...  156 us

profile of v3, /device:TPU:0, one launch (start us, length us, event | category | flops | bytes accessed | tf_op | source)
XLA Modules:
  0.0 159.2 jit_solution(1439485320828261105)
XLA Ops:
  0.6 155.8 %shard_map.229 = (bf16[256,768]{1,0:T(8,128)(2,1)}, bf16[256,768]{1,0:T(8,128)(2,1)}, f32[48,384]{1,0:T(8,128)}, f32[48,384]{1,0:T(8,128)}, f32[48,384]{1,0:T(8,...) custom-call(bf16[256,768]{1,0:T(8,128)(2,1)} %refs_0_.1, ...), custom_call_target="tpu_custom_call" | custom-call | tf_op jit(solution)/shard_map/pallas_call | solution.py:754
  156.4 2.6 %shard_map.230 = (bf16[256,768]{1,0:T(8,128)(2,1)}, bf16[256,768]{1,0:T(8,128)(2,1)}, f32[48,384]{1,0:T(8,128)}, f32[48,384]{1,0:T(8,128)}, f32[48,384]{1,0:T(8,...) custom-call(bf16[256,768]{1,0:T(8,128)(2,1)} %get-tuple-element.36.r, ...), custom_call_target="tpu_custom_call" | custom-call | tf_op jit(solution)/shard_map/pallas_call | solution.py:764

commit v4 on v3

--- a/solution.py
+++ b/solution.py
@@ -24,7 +24,7 @@
 PER_PIECE = ("G", "S1", "R1", "S2A", "R2A", "S3A", "R3A", "S2C", "R2C", "S3C", "R3C")
 DP, HEAD = "dp", "head"
 BOTH = (DP, HEAD)
-COPIES = 200
+COPIES = 202
 
 
 def mm(a, b, ca=1, cb=0):
@@ -33,6 +33,8 @@
 
 def scratch_list():
     items = []
+    for name, shape, dtype in MOVED_IN + MOVED_OUT:
+        items.append((name, pltpu.VMEM(shape, dtype)))
 
     def add(name, shape, dtype):
         items.append((name, pltpu.VMEM(shape, dtype)))
@@ -78,16 +80,46 @@
     add("VR", (80, 768), F32)
     items.append(("ss", pltpu.SemaphoreType.DMA((COPIES,))))
     items.append(("rs", pltpu.SemaphoreType.DMA((COPIES,))))
-    items.append(("ls", pltpu.SemaphoreType.DMA((1,))))
+    items.append(("ls", pltpu.SemaphoreType.DMA((1 + len(MOVED_IN) + len(MOVED_OUT),))))
     return items
 
 
 IN_NAMES = ("tok", "wq", "wk", "wv", "wo", "ga", "ba", "wu", "wd", "gf", "bf", "len", "off", "og")
+MOVED_IN = (
+    ("wq", (48, 384), F32),
+    ("wk", (48, 384), F32),
+    ("wv", (48, 384), F32),
+    ("ga", (24,), F32),
+    ("ba", (24,), F32),
+    ("gf", (24,), F32),
+    ("bf", (24,), F32),
+    ("tok", (256, 768), BF),
+    ("wo", (24, 768), F32),
+    ("wu", (96, 768), F32),
+    ("wd", (96, 768), F32),
+    ("og", (256, 768), BF),
+)
+MOVED_OUT = (
+    ("out", (256, 768), BF),
+    ("ig", (256, 768), BF),
+    ("dwq", (48, 384), F32),
+    ("dwk", (48, 384), F32),
+    ("dwv", (48, 384), F32),
+    ("dwo", (24, 768), F32),
+    ("dga", (24,), F32),
+    ("dba", (24,), F32),
+    ("dwu", (96, 768), F32),
+    ("dwd", (96, 768), F32),
+    ("dgf", (24,), F32),
+    ("dbf", (24,), F32),
+)
 OUT_NAMES = ("out", "ig", "dwq", "dwk", "dwv", "dwo", "dga", "dba", "dwu", "dwd", "dgf", "dbf")
 
 
 def layer_kernel(*refs):
-    names = IN_NAMES + OUT_NAMES + tuple(n for n, _ in scratch_list())
+    ins = tuple(n if n in ("len", "off") else "far_" + n for n in IN_NAMES)
+    outs = tuple("far_" + n for n in OUT_NAMES)
+    names = ins + outs + tuple(n for n, _ in scratch_list())
     named = dict(zip(names, refs))
     r = types.SimpleNamespace(**named)
     for key in PER_PIECE:
@@ -115,6 +147,22 @@
     own_rows = pl.ds(pl.multiple_of(256 * c, 256), 256)
     oth_rows = pl.ds(pl.multiple_of(256 * (1 - c), 256), 256)
 
+    in_copies, out_copies = {}, []
+    for k, (n, _, _) in enumerate(MOVED_IN):
+        in_copies[n] = pltpu.make_async_copy(named["far_" + n], named[n], r.ls.at[1 + k])
+        in_copies[n].start()
+
+    def arrived(*keys):
+        for n in keys:
+            in_copies[n].wait()
+
+    def put(*keys):
+        for n in keys:
+            k = 1 + len(MOVED_IN) + OUT_NAMES.index(n)
+            cp = pltpu.make_async_copy(named[n], named["far_" + n], r.ls.at[k])
+            cp.start()
+            out_copies.append(cp)
+
     peers = [partner] + [(ids[m], c) for m in (MU, MV, 4, 8, 12)]
     barrier = pltpu.get_barrier_semaphore()
     for dev in peers:
@@ -236,8 +284,8 @@
             s()
 
     vec_peers = (
-        (partner, (ids[MU], c), (ids[MV], c), (ids[4], c), (ids[8], c)),
-        (partner, (ids[4], c), (ids[8], c), (ids[MU], c), (ids[MV], c)),
+        ((ids[4], c), (ids[8], c), (ids[MV], c), (ids[MU], c), partner),
+        ((ids[MV], c), (ids[MU], c), (ids[4], c), (ids[8], c), partner),
     )
 
     def vec_send(k, s):
@@ -338,28 +386,37 @@
             near = pl.ds(pl.multiple_of(base + block_row(zm, du, 0) * rows, 8), rows)
             r.S1[p][k : k + rows, :] = src[far, 0:cols].astype(BF)
             r.G[p][k : k + rows, :] = src[near, 0:cols]
-        rs1_send(p, zm)
-
-    r.WQ[pl.ds(pl.multiple_of(me * 48, 16), 48), 0:384] = r.wq[...].astype(BF)
-    r.WQ[pl.ds(pl.multiple_of(me * 48, 16), 48), 384:768] = r.wk[...].astype(BF)
-    r.WQ[pl.ds(pl.multiple_of(me * 48, 16), 48), 768:1152] = r.wv[...].astype(BF)
-    ag_own("Q")
-    send("tok", r.tok, r.X.at[own_rows, :], partner)
-    local = pltpu.make_async_copy(r.tok, r.X.at[own_rows, :], r.ls.at[0])
-    local.start()
+
     flat = 2 * me + c
+    arrived("ga", "ba", "gf", "bf")
     r.VS[0:8, :] = jnp.zeros((8, 768), F32)
     for k, n in enumerate(("ga", "ba", "gf", "bf")):
         r.VS[k : k + 1, 0:24] = getattr(r, n)[...].reshape(1, 24).astype(BF).astype(F32)
     r.VS[0:8, :] = pltpu.roll(r.VS[0:8, :], 24 * flat, 1)
     vec_send(0, 0)
+    arrived("wq", "wk", "wv")
+    r.WQ[pl.ds(pl.multiple_of(me * 48, 16), 48), 0:384] = r.wq[...].astype(BF)
+    r.WQ[pl.ds(pl.multiple_of(me * 48, 16), 48), 384:768] = r.wk[...].astype(BF)
+    r.WQ[pl.ds(pl.multiple_of(me * 48, 16), 48), 768:1152] = r.wv[...].astype(BF)
+    ag_own("Q")
+    arrived("tok")
+    send("tok", r.tok, r.X.at[own_rows, :], partner)
+    local = pltpu.make_async_copy(r.tok, r.X.at[own_rows, :], r.ls.at[0])
+    local.start()
+    arrived("wo")
     wo = r.wo[...]
     r.WOP[c, pl.ds(pl.multiple_of(me * 48, 16), 48), :] = jnp.concatenate(
         [wo[:, 0:384], wo[:, 384:768]], axis=0
     ).astype(BF)
-    ag_own("O")
+    arrived("wu", "wd", "og")
     r.WU[pl.ds(pl.multiple_of(me * 96, 16), 96), :] = r.wu[...].astype(BF)
     r.WD[pl.ds(pl.multiple_of(me * 96, 16), 96), :] = r.wd[...].astype(BF)
+
+    q_steps, o_steps, u_steps, d_steps = (ag_steps(p) for p in PIECES)
+    run(q_steps[:5])
+    ag_own("O")
+    vec_step(0, 0)
+    run(o_steps[:1])
 
     col_pos = lax.broadcasted_iota(jnp.int32, (512, 128), 0)
     row_pos = lax.broadcasted_iota(jnp.int32, (8, 512), 1)
@@ -378,13 +435,10 @@
         same = lab == jnp.broadcast_to(row_lab[0:1], (128, 512))
         r.BIAS[q, :] = jnp.where(same, 0.0, -1e30).astype(F32)
 
-    q_steps, o_steps, u_steps, d_steps = (ag_steps(p) for p in PIECES)
-    run(q_steps[:5])
+    run(q_steps[5:])
+    vec_step(0, 1)
+    run(o_steps[1:5])
     ag_own("U")
-    vec_step(0, 0)
-    run(o_steps[:5])
-    run(q_steps[5:])
-    ag_own("D")
     wait_recv("tok", r.X.at[own_rows, :])
     local.wait()
     for zm in range(4):
@@ -397,18 +451,18 @@
             full = full * BF(0.125)
         for i in range(3):
             getattr(r, n)[i] = full[:, 128 * i : 128 * i + 128]
-    vec_step(0, 1)
-    run(u_steps[:2])
+    vec_step(0, 2)
+    run(u_steps[:1])
 
     for i in range(3):
         r.ATT[i] = jnp.zeros((512, 128), BF)
     fw_hooks = [
-        u_steps[2:5],
-        [functools.partial(vec_step, 0, 2)] + o_steps[5:8],
-        o_steps[8:12],
-        o_steps[12:] + d_steps[:1] + [functools.partial(vec_step, 0, 3)],
-        d_steps[1:3],
-        d_steps[3:5],
+        o_steps[5:8],
+        o_steps[8:],
+        [functools.partial(vec_step, 0, 3)] + u_steps[1:3],
+        u_steps[3:5],
+        u_steps[5:8],
+        u_steps[8:10],
     ]
     lane = lax.broadcasted_iota(jnp.int32, (1, 128), 1)
 
@@ -446,10 +500,11 @@
     lax.fori_loop(0, 6, fwd_head, 0)
 
     send("att", r.ATT.at[:, oth_rows, :], r.ATTR, partner)
+    ag_own("D")
     for zm in range(4):
         ag_plane("O", zm)
     send("wop", r.WOP.at[c], r.WOP.at[c], partner)
-    run(u_steps[5:8])
+    run(d_steps[:1] + u_steps[10:12])
     vec_step(0, 4)
     wait_recv("wop", r.WOP.at[1 - c])
 
@@ -473,7 +528,7 @@
     branch = mm(joined(r.ATT, own_rows), r.WO[own_heads, :])
     branch = branch + mm(joined(r.ATTR, all256), r.WO[oth_heads, :])
     r.GS[...] = branch
-    run(u_steps[8:11])
+    run(u_steps[12:] + d_steps[1:2])
 
     def norm(val):
         mean = jnp.mean(val, axis=1, keepdims=True)
@@ -493,7 +548,7 @@
 
     lax.fori_loop(0, 4, ln1, 0)
     send("fin", r.FIN.at[own_rows, :], r.FIN.at[own_rows, :], partner)
-    run(u_steps[11:])
+    run(d_steps[2:5])
     wait_recv("fin", r.FIN.at[oth_rows, :])
 
     def plane_rows(zm):
@@ -516,11 +571,11 @@
 
         lax.fori_loop(0, 8, act, 0)
 
-    d_groups = (d_steps[5:8], d_steps[8:11], d_steps[11:], [])
+    d_groups = ([], d_steps[5:8], d_steps[8:11], d_steps[11:])
     for zm in range(4):
         ag_plane("U", zm)
+        run(d_groups[zm])
         ffn_up(zm)
-        run(d_groups[zm])
     for zm in range(4):
         ag_plane("D", zm)
         for rows in (oth_rows, own_rows):
@@ -529,8 +584,9 @@
                 part = part + r.SEC[rows, :]
             r.SEC[rows, :] = part
             if zm == 3 and rows is oth_rows:
-                send("sec", r.SEC.at[oth_rows, :], r.SECR, partner)
-    wait_recv("sec", r.SECR)
+                for h in range(2):
+                    part_rows = pl.ds(pl.multiple_of(256 * (1 - c) + 128 * h, 128), 128)
+                    send(("sec", h), r.SEC.at[part_rows, :], r.SECR.at[pl.ds(128 * h, 128), :], partner)
 
     def ln2(t, sums):
         dg, db = sums
@@ -550,20 +606,35 @@
         return dg, db
 
     zero = jnp.zeros((1, 768), F32)
-    dg2, db2 = lax.fori_loop(0, 4, ln2, (zero, zero))
-    send("gfb", r.GFB.at[own_rows, :], r.GFB.at[own_rows, :], partner)
-    wait_recv("gfb", r.GFB.at[oth_rows, :])
-    wait_sent("sec")
+    dg2, db2 = zero, zero
+    for h in range(2):
+        wait_recv(("sec", h), r.SECR.at[pl.ds(128 * h, 128), :])
+        dg2, db2 = lax.fori_loop(2 * h, 2 * h + 2, ln2, (dg2, db2))
+        part_rows = r.GFB.at[pl.ds(pl.multiple_of(base256 + 128 * h, 128), 128), :]
+        send(("gfb", h), part_rows, part_rows, partner)
+    put("out")
+    r.T[0:384, 0:768] = mm(r.HID[3, own_rows, :], r.GFB[own_rows, :], 0, 0)
+    for h in range(2):
+        wait_recv(("gfb", h), r.GFB.at[pl.ds(pl.multiple_of(256 * (1 - c) + 128 * h, 128), 128), :])
+    for h in range(2):
+        wait_sent(("sec", h))
 
     for n_done, zm in enumerate((3, 2, 1, 0)):
-        r.T[0:384, 0:768] = mm(r.HID[zm], r.GFB[...], 0, 0)
+        if zm == 3:
+            r.T[0:384, 0:768] = r.T[0:384, 0:768] + mm(r.HID[3, oth_rows, :], r.GFB[oth_rows, :], 0, 0)
+        else:
+            r.T[0:384, 0:768] = mm(r.HID[zm], r.GFB[...], 0, 0)
         stage("D", zm, r.T, 0)
+        if zm:
+            rs1_send("D", zm)
         for t in range(2):
             q = slice(256 * t, 256 * t + 256)
             gh = mm(r.GFB[q, :], r.WD[plane_rows(zm), :], 1, 1)
             r.HID[zm, q, :] = (gh * r.GEL[zm, q, :]).astype(BF)
         r.T[384:768, 0:768] = mm(r.HID[zm], r.FIN[...], 0, 0)
         stage("U", zm, r.T, 384)
+        if zm > 1:
+            rs1_send("U", zm)
         for rows in (oth_rows, own_rows):
             part = mm(r.HID[zm, rows, :], r.WU[plane_rows(zm), :])
             if n_done:
@@ -605,8 +676,7 @@
     gview = mm(r.GB[...], r.WO[own_heads, :], 1, 1).astype(BF)
     for i in range(3):
         r.GA[i, own_rows, :] = gview[:, 128 * i : 128 * i + 128]
-    vec_step(1, 0)
-    rs_sum1("D", 2)
+    rs_sum2a("D", 3)
     r.T[own_heads, 0:768] = mm(joined(r.ATT, own_rows), r.GB[...], 0, 0)
     r.T[oth_heads, 0:768] = mm(joined(r.ATTR, all256), r.GB[...], 0, 0)
 
@@ -618,7 +688,8 @@
 
     lax.fori_loop(0, 16, pair_out, 0)
     send("s0", r.S0, r.R0, partner)
-    rs_sum2a("D", 3)
+    rs_sum1("D", 2)
+    rs_sum2a("U", 3)
     wait_recv("s0", r.R0)
 
     def out_block(m):
@@ -632,7 +703,9 @@
             k = (2 * zm + du) * 48
             r.S1["O"][k : k + 48, :] = out_block(4 * zm + 2 * du + 1).astype(BF)
             r.G["O"][k : k + 48, :] = out_block(4 * zm + 2 * du)
-        rs1_send("O", zm)
+        if zm > 1:
+            rs1_send("O", zm)
+    rs1_send("U", 1)
 
     wait_recv("gas", r.GA.at[:, oth_rows, :])
     for n in ("DQ", "DK", "DV"):
@@ -652,12 +725,12 @@
         return functools.partial(vec_step, 1, s)
 
     bw_hooks = [
-        [s2a("U", 3), vs(1)],
+        [],
         [s1("U", 2)],
-        [s2a("D", 2), vs(2)],
+        [s2a("D", 2)],
+        [],
         [s1("D", 1)],
-        [s2a("U", 2), vs(3)],
-        [],
+        [s2a("U", 2), vs(0)],
     ]
 
     def bwd_head(h, carry):
@@ -686,7 +759,11 @@
         r.T[:, 384 * k : 384 * k + 384] = mm(r.X[...], joined(getattr(r, n), all512), 0, 0)
     for zm in (3, 2, 1, 0):
         stage("Q", zm, r.T, 192 * zs[zm])
-    run([s1("U", 1), s2a("D", 1)])
+        if zm:
+            rs1_send("Q", zm)
+    for p, zm in (("O", 1), ("Q", 0), ("D", 0), ("U", 0), ("O", 0)):
+        rs1_send(p, zm)
+    run([s2a("D", 1), s1("O", 3), vs(1), s1("O", 2)])
 
     for rows in (oth_rows, own_rows):
         acc = mm(joined(r.DQ, rows), r.WQ[:, 0:384], 1, 1)
@@ -695,34 +772,39 @@
         if rows is oth_rows:
             r.IGS[...] = acc.astype(BF)
             send("ig", r.IGS, r.IGR, partner)
-            run([s1("D", 0), s2a("U", 1)])
+            run([s2a("O", 3), s2a("O", 2), s1("U", 1), vs(2)])
         else:
             r.GS[...] = r.GS[...] + acc
     wait_recv("ig", r.IGR)
     r.ig[...] = (r.GS[...] + r.IGR[...].astype(F32)).astype(BF)
-
-    run([s1("U", 0), s2a("D", 0), s2c("D"), s2a("U", 0), s2c("U")])
-    run([s1("O", 3), s1("O", 2), s2a("O", 3), s1("O", 1), s2a("O", 2), s1("O", 0)])
-    run([s2a("O", 1), s2a("O", 0), vs(4), s2c("O")])
-    run([s1("Q", 3), s1("Q", 2), s2a("Q", 3), s1("Q", 1), s2a("Q", 2), s1("Q", 0)])
-    run([s2a("Q", 1), s2a("Q", 0), s2c("Q")])
-    for p in ("D", "U", "O"):
-        rs_final(p)
+    put("ig")
+
+    run([s1("Q", 3), s2a("U", 1), s1("Q", 2), s2a("Q", 3), s1("Q", 1), s2a("Q", 2), vs(3)])
+    run([s1("O", 1), s2a("Q", 1), s1("Q", 0), s2c("Q"), s2a("O", 1)])
+    run([s1("D", 0), s2c("D"), s2a("Q", 0), s1("U", 0), s2c("U"), s2a("D", 0)])
+    run([s1("O", 0), s2c("O"), s2a("U", 0), s2a("O", 0), vs(4)])
+    rs_final("Q")
+    r.dwq[...] = r.G["Q"][0:48, 0:384]
+    r.dwk[...] = r.G["Q"][0:48, 384:768]
+    r.dwv[...] = r.G["Q"][0:48, 768:1152]
+    rs_final("D")
     r.dwd[...] = r.G["D"][0:96, :]
+    put("dwq", "dwk", "dwv", "dwd")
+    rs_final("U")
     r.dwu[...] = r.G["U"][0:96, :]
+    rs_final("O")
     go = r.G["O"][0:48, :]
     r.dwo[...] = jnp.concatenate([go[0:24], go[24:48]], axis=1)
     back = pltpu.roll(r.VS[88:96, :], lax.rem(768 - 24 * flat, 768), 1)
     for k, n in enumerate(("dga", "dba", "dgf", "dbf")):
         getattr(r, n)[...] = back[k, 0:24]
-    rs_final("Q")
-    r.dwq[...] = r.G["Q"][0:48, 0:384]
-    r.dwk[...] = r.G["Q"][0:48, 384:768]
-    r.dwv[...] = r.G["Q"][0:48, 768:1152]
+    put("dwu", "dwo", "dga", "dba", "dgf", "dbf")
 
     for entry in sends:
         if entry[3] not in waited:
             wait_send(entry)
+    for cp in out_copies:
+        cp.wait()
 
 
 def hand_over(*refs):
@@ -732,30 +814,18 @@
 
 
 def layer_small(*args):
-    shapes = (
-        ((256, 768), BF),
-        ((256, 768), BF),
-        ((48, 384), F32),
-        ((48, 384), F32),
-        ((48, 384), F32),
-        ((24, 768), F32),
-        ((24,), F32),
-        ((24,), F32),
-        ((96, 768), F32),
-        ((96, 768), F32),
-        ((24,), F32),
-        ((24,), F32),
-    )
+    shapes = tuple((shape, dtype) for _, shape, dtype in MOVED_OUT)
     vmem = pl.BlockSpec(memory_space=pltpu.VMEM)
     smem = pl.BlockSpec(memory_space=pltpu.SMEM)
+    anywhere = pl.BlockSpec(memory_space=pl.ANY)
     out_shape = tuple(jax.ShapeDtypeStruct(s, d) for s, d in shapes)
     up = IN_NAMES.index("wu")
     args = args[:up] + (args[up].T,) + args[up + 1 :]
     outs = pl.pallas_call(
         layer_kernel,
         out_shape=out_shape,
-        in_specs=[smem if n in ("len", "off") else vmem for n in IN_NAMES],
-        out_specs=tuple(vmem for _ in shapes),
+        in_specs=[smem if n in ("len", "off") else anywhere for n in IN_NAMES],
+        out_specs=tuple(anywhere for _ in shapes),
         scratch_shapes=[s for _, s in scratch_list()],
         compiler_params=pltpu.CompilerParams(
             collective_id=0, has_side_effects=True, vmem_limit_bytes=67043328

time: 159 us -> 147 us (0.925)
  Pallas kernels: 158 us -> 146 us
    pallas_call x1, Pallas kernels: 156 us -> 143 us  [layer_small(): pl.pallas_call(layer_kernel, out_shape=out_shape, in_specs=[smem if n in...]
where the time goes in v4:
time: 147 us
  Pallas kernels  146 us (99%)
    pallas_call x1, Pallas kernels, layer_small(): pl.pallas_call(layer_kernel, out_shape=out_shape, in_specs=[smem if n in...  143 us

profile of v4, /device:TPU:0, one launch (start us, length us, event | category | flops | bytes accessed | tf_op | source)
XLA Modules:
  0.0 146.9 jit_solution(12851353383543993081)
XLA Ops:
  0.6 143.5 %shard_map.229 = (bf16[256,768]{1,0:T(8,128)(2,1)}, bf16[256,768]{1,0:T(8,128)(2,1)}, f32[48,384]{1,0:T(8,128)}, f32[48,384]{1,0:T(8,128)}, f32[48,384]{1,0:T(8,...) custom-call(bf16[256,768]{1,0:T(8,128)(2,1)} %refs_0_.1, ...), custom_call_target="tpu_custom_call" | custom-call | tf_op jit(solution)/shard_map/pallas_call | solution.py:824
  144.1 2.6 %shard_map.230 = (bf16[256,768]{1,0:T(8,128)(2,1)}, bf16[256,768]{1,0:T(8,128)(2,1)}, f32[48,384]{1,0:T(8,128)}, f32[48,384]{1,0:T(8,128)}, f32[48,384]{1,0:T(8,...) custom-call(bf16[256,768]{1,0:T(8,128)(2,1)} %get-tuple-element.36.r, ...), custom_call_target="tpu_custom_call" | custom-call | tf_op jit(solution)/shard_map/pallas_call | solution.py:834

commit v5 on v4

--- a/solution.py
+++ b/solution.py
@@ -24,7 +24,7 @@
 PER_PIECE = ("G", "S1", "R1", "S2A", "R2A", "S3A", "R3A", "S2C", "R2C", "S3C", "R3C")
 DP, HEAD = "dp", "head"
 BOTH = (DP, HEAD)
-COPIES = 202
+COPIES = 204
 
 
 def mm(a, b, ca=1, cb=0):
@@ -77,7 +77,7 @@
         for key, size in zip(PER_PIECE, sizes):
             add(key + p, (size, c), F32 if key == "G" else BF)
     add("VS", (96, 768), F32)
-    add("VR", (80, 768), F32)
+    add("VR", (96, 768), F32)
     items.append(("ss", pltpu.SemaphoreType.DMA((COPIES,))))
     items.append(("rs", pltpu.SemaphoreType.DMA((COPIES,))))
     items.append(("ls", pltpu.SemaphoreType.DMA((1 + len(MOVED_IN) + len(MOVED_OUT),))))
@@ -283,19 +283,25 @@
         for s in steps:
             s()
 
-    vec_peers = (
-        ((ids[4], c), (ids[8], c), (ids[MV], c), (ids[MU], c), partner),
-        ((ids[MV], c), (ids[MU], c), (ids[4], c), (ids[8], c), partner),
-    )
+    flip_u, flip_v = ((ids[MU], c),), ((ids[MV], c),)
+    line = tuple((ids[m], c) for m in (4, 8, 12))
+    vec_peers = ((line, flip_v, flip_u, (partner,)), ((partner,), flip_v, flip_u, line))
+
+    def vec_slots(k, s):
+        first = 48 * k + 8 * (s + (2 if k == 0 and s else 0))
+        return [pl.ds(first + 8 * j, 8) for j in range(len(vec_peers[k][s]))]
 
     def vec_send(k, s):
-        send(("v", k, s), r.VS.at[pl.ds(48 * k + 8 * s, 8), :], r.VR.at[pl.ds(40 * k + 8 * s, 8), :], vec_peers[k][s])
+        for j, (slot, dev) in enumerate(zip(vec_slots(k, s), vec_peers[k][s])):
+            send(("v", k, s, j), r.VS.at[pl.ds(48 * k + 8 * s, 8), :], r.VR.at[slot, :], dev)
 
     def vec_step(k, s):
-        src, got_row = pl.ds(48 * k + 8 * s, 8), pl.ds(40 * k + 8 * s, 8)
-        wait_recv(("v", k, s), r.VR.at[got_row, :])
-        r.VS[pl.ds(48 * k + 8 * s + 8, 8), :] = r.VS[src, :] + r.VR[got_row, :]
-        if s < 4:
+        total = r.VS[pl.ds(48 * k + 8 * s, 8), :]
+        for j, slot in enumerate(vec_slots(k, s)):
+            wait_recv(("v", k, s, j), r.VR.at[slot, :])
+            total = total + r.VR[slot, :]
+        r.VS[pl.ds(48 * k + (8 * s + 8 if s < 3 else 40), 8), :] = total
+        if s < 3:
             vec_send(k, s + 1)
 
     def rs1_send(p, zm):
@@ -388,12 +394,6 @@
             r.G[p][k : k + rows, :] = src[near, 0:cols]
 
     flat = 2 * me + c
-    arrived("ga", "ba", "gf", "bf")
-    r.VS[0:8, :] = jnp.zeros((8, 768), F32)
-    for k, n in enumerate(("ga", "ba", "gf", "bf")):
-        r.VS[k : k + 1, 0:24] = getattr(r, n)[...].reshape(1, 24).astype(BF).astype(F32)
-    r.VS[0:8, :] = pltpu.roll(r.VS[0:8, :], 24 * flat, 1)
-    vec_send(0, 0)
     arrived("wq", "wk", "wv")
     r.WQ[pl.ds(pl.multiple_of(me * 48, 16), 48), 0:384] = r.wq[...].astype(BF)
     r.WQ[pl.ds(pl.multiple_of(me * 48, 16), 48), 384:768] = r.wk[...].astype(BF)
@@ -403,6 +403,12 @@
     send("tok", r.tok, r.X.at[own_rows, :], partner)
     local = pltpu.make_async_copy(r.tok, r.X.at[own_rows, :], r.ls.at[0])
     local.start()
+    arrived("ga", "ba", "gf", "bf")
+    r.VS[0:8, :] = jnp.zeros((8, 768), F32)
+    for k, n in enumerate(("ga", "ba", "gf", "bf")):
+        r.VS[k : k + 1, 0:24] = getattr(r, n)[...].reshape(1, 24).astype(BF).astype(F32)
+    r.VS[0:8, :] = pltpu.roll(r.VS[0:8, :], 24 * flat, 1)
+    vec_send(0, 0)
     arrived("wo")
     wo = r.wo[...]
     r.WOP[c, pl.ds(pl.multiple_of(me * 48, 16), 48), :] = jnp.concatenate(
@@ -415,7 +421,6 @@
     q_steps, o_steps, u_steps, d_steps = (ag_steps(p) for p in PIECES)
     run(q_steps[:5])
     ag_own("O")
-    vec_step(0, 0)
     run(o_steps[:1])
 
     col_pos = lax.broadcasted_iota(jnp.int32, (512, 128), 0)
@@ -436,7 +441,7 @@
         r.BIAS[q, :] = jnp.where(same, 0.0, -1e30).astype(F32)
 
     run(q_steps[5:])
-    vec_step(0, 1)
+    vec_step(0, 0)
     run(o_steps[1:5])
     ag_own("U")
     wait_recv("tok", r.X.at[own_rows, :])
@@ -451,15 +456,15 @@
             full = full * BF(0.125)
         for i in range(3):
             getattr(r, n)[i] = full[:, 128 * i : 128 * i + 128]
-    vec_step(0, 2)
     run(u_steps[:1])
+    vec_step(0, 1)
 
     for i in range(3):
         r.ATT[i] = jnp.zeros((512, 128), BF)
     fw_hooks = [
         o_steps[5:8],
         o_steps[8:],
-        [functools.partial(vec_step, 0, 3)] + u_steps[1:3],
+        [functools.partial(vec_step, 0, 2)] + u_steps[1:3],
         u_steps[3:5],
         u_steps[5:8],
         u_steps[8:10],
@@ -505,7 +510,7 @@
         ag_plane("O", zm)
     send("wop", r.WOP.at[c], r.WOP.at[c], partner)
     run(d_steps[:1] + u_steps[10:12])
-    vec_step(0, 4)
+    vec_step(0, 3)
     wait_recv("wop", r.WOP.at[1 - c])
 
     def build_out(i, carry):
@@ -625,7 +630,7 @@
         else:
             r.T[0:384, 0:768] = mm(r.HID[zm], r.GFB[...], 0, 0)
         stage("D", zm, r.T, 0)
-        if zm:
+        if zm > 1:
             rs1_send("D", zm)
         for t in range(2):
             q = slice(256 * t, 256 * t + 256)
@@ -645,6 +650,7 @@
         if n_done == 2:
             rs_sum1("D", 3)
     rs_sum1("U", 3)
+    rs1_send("D", 1)
     wait_recv("gn", r.SECR)
 
     def ln1_back(t, sums):
@@ -676,7 +682,9 @@
     gview = mm(r.GB[...], r.WO[own_heads, :], 1, 1).astype(BF)
     for i in range(3):
         r.GA[i, own_rows, :] = gview[:, 128 * i : 128 * i + 128]
+    vec_step(1, 0)
     rs_sum2a("D", 3)
+    rs1_send("U", 1)
     r.T[own_heads, 0:768] = mm(joined(r.ATT, own_rows), r.GB[...], 0, 0)
     r.T[oth_heads, 0:768] = mm(joined(r.ATTR, all256), r.GB[...], 0, 0)
 
@@ -705,7 +713,6 @@
             r.G["O"][k : k + 48, :] = out_block(4 * zm + 2 * du)
         if zm > 1:
             rs1_send("O", zm)
-    rs1_send("U", 1)
 
     wait_recv("gas", r.GA.at[:, oth_rows, :])
     for n in ("DQ", "DK", "DV"):
@@ -730,7 +737,7 @@
         [s2a("D", 2)],
         [],
         [s1("D", 1)],
-        [s2a("U", 2), vs(0)],
+        [s2a("U", 2), vs(1)],
     ]
 
     def bwd_head(h, carry):
@@ -759,11 +766,13 @@
         r.T[:, 384 * k : 384 * k + 384] = mm(r.X[...], joined(getattr(r, n), all512), 0, 0)
     for zm in (3, 2, 1, 0):
         stage("Q", zm, r.T, 192 * zs[zm])
-        if zm:
+        if zm > 1:
             rs1_send("Q", zm)
-    for p, zm in (("O", 1), ("Q", 0), ("D", 0), ("U", 0), ("O", 0)):
-        rs1_send(p, zm)
-    run([s2a("D", 1), s1("O", 3), vs(1), s1("O", 2)])
+
+    def s0(p, zm):
+        return functools.partial(rs1_send, p, zm)
+
+    run([s1("U", 1), s2a("D", 1), vs(2), s0("Q", 1), s0("O", 1)])
 
     for rows in (oth_rows, own_rows):
         acc = mm(joined(r.DQ, rows), r.WQ[:, 0:384], 1, 1)
@@ -772,17 +781,17 @@
         if rows is oth_rows:
             r.IGS[...] = acc.astype(BF)
             send("ig", r.IGS, r.IGR, partner)
-            run([s2a("O", 3), s2a("O", 2), s1("U", 1), vs(2)])
+            run([s1("O", 3), s1("O", 2), s2a("U", 1), s2a("O", 3), s0("D", 0)])
         else:
             r.GS[...] = r.GS[...] + acc
     wait_recv("ig", r.IGR)
     r.ig[...] = (r.GS[...] + r.IGR[...].astype(F32)).astype(BF)
     put("ig")
 
-    run([s1("Q", 3), s2a("U", 1), s1("Q", 2), s2a("Q", 3), s1("Q", 1), s2a("Q", 2), vs(3)])
-    run([s1("O", 1), s2a("Q", 1), s1("Q", 0), s2c("Q"), s2a("O", 1)])
-    run([s1("D", 0), s2c("D"), s2a("Q", 0), s1("U", 0), s2c("U"), s2a("D", 0)])
-    run([s1("O", 0), s2c("O"), s2a("U", 0), s2a("O", 0), vs(4)])
+    run([s1("Q", 3), s2a("O", 2), s0("U", 0), s1("Q", 2), s2a("Q", 3), s0("Q", 0)])
+    run([s1("Q", 1), s2a("Q", 2), s1("O", 1), s2a("Q", 1), s1("D", 0), s2a("O", 1), s2c("D")])
+    run([s1("U", 0), s2c("U"), s2a("D", 0), s0("O", 0), s1("Q", 0), s2c("Q"), s2a("U", 0)])
+    run([s2a("Q", 0), s1("O", 0), s2c("O"), s2a("O", 0)])
     rs_final("Q")
     r.dwq[...] = r.G["Q"][0:48, 0:384]
     r.dwk[...] = r.G["Q"][0:48, 384:768]
@@ -793,6 +802,7 @@
     rs_final("U")
     r.dwu[...] = r.G["U"][0:96, :]
     rs_final("O")
+    vec_step(1, 3)
     go = r.G["O"][0:48, :]
     r.dwo[...] = jnp.concatenate([go[0:24], go[24:48]], axis=1)
     back = pltpu.roll(r.VS[88:96, :], lax.rem(768 - 24 * flat, 768), 1)

time: 147 us -> 145 us (0.986)
  Pallas kernels: 146 us -> 144 us
    pallas_call x1, Pallas kernels: 143 us -> 141 us  [layer_small(): pl.pallas_call(layer_kernel, out_shape=out_shape, in_specs=[smem if n in...]
where the time goes in v5:
time: 145 us; the launch traced here: 144 us
  Pallas kernels  144 us (99%)
    pallas_call x1, Pallas kernels, layer_small(): pl.pallas_call(layer_kernel, out_shape=out_shape, in_specs=[smem if n in...  141 us

profile of v5, /device:TPU:0, one launch (start us, length us, event | category | flops | bytes accessed | tf_op | source)
XLA Modules:
  0.0 144.5 jit_solution(5462225096464999747)
XLA Ops:
  0.6 141.0 %shard_map.229 = (bf16[256,768]{1,0:T(8,128)(2,1)}, bf16[256,768]{1,0:T(8,128)(2,1)}, f32[48,384]{1,0:T(8,128)}, f32[48,384]{1,0:T(8,128)}, f32[48,384]{1,0:T(8,...) custom-call(bf16[256,768]{1,0:T(8,128)(2,1)} %refs_0_.1, ...), custom_call_target="tpu_custom_call" | custom-call | tf_op jit(solution)/shard_map/pallas_call | solution.py:834
  141.7 2.6 %shard_map.230 = (bf16[256,768]{1,0:T(8,128)(2,1)}, bf16[256,768]{1,0:T(8,128)(2,1)}, f32[48,384]{1,0:T(8,128)}, f32[48,384]{1,0:T(8,128)}, f32[48,384]{1,0:T(8,...) custom-call(bf16[256,768]{1,0:T(8,128)(2,1)} %get-tuple-element.36.r, ...), custom_call_target="tpu_custom_call" | custom-call | tf_op jit(solution)/shard_map/pallas_call | solution.py:844

commit v6 on v5

--- a/solution.py
+++ b/solution.py
@@ -24,7 +24,7 @@
 PER_PIECE = ("G", "S1", "R1", "S2A", "R2A", "S3A", "R3A", "S2C", "R2C", "S3C", "R3C")
 DP, HEAD = "dp", "head"
 BOTH = (DP, HEAD)
-COPIES = 204
+SENT, RECEIVED = 52, 140
 
 
 def mm(a, b, ca=1, cb=0):
@@ -78,8 +78,8 @@
             add(key + p, (size, c), F32 if key == "G" else BF)
     add("VS", (96, 768), F32)
     add("VR", (96, 768), F32)
-    items.append(("ss", pltpu.SemaphoreType.DMA((COPIES,))))
-    items.append(("rs", pltpu.SemaphoreType.DMA((COPIES,))))
+    items.append(("ss", pltpu.SemaphoreType.DMA((SENT,))))
+    items.append(("rs", pltpu.SemaphoreType.DMA((RECEIVED,))))
     items.append(("ls", pltpu.SemaphoreType.DMA((1 + len(MOVED_IN) + len(MOVED_OUT),))))
     return items
 
@@ -170,50 +170,48 @@
     pl.semaphore_wait(barrier, len(peers))
 
     sends = []
-    recv_ids = {}
-
-    def recv_sem(key):
-        if key not in recv_ids:
-            recv_ids[key] = len(recv_ids)
-        return r.rs.at[recv_ids[key]]
-
-    def send(key, src, dst, dev):
+    send_ids, recv_ids = {}, {}
+
+    def sem_of(sems, ids_of, name):
+        return sems.at[ids_of.setdefault(name, len(ids_of))]
+
+    def send(key, src, dst, dev, out_group=None, in_group=None):
+        out = out_group or ("one", len(sends))
         cp = pltpu.make_async_remote_copy(
             src_ref=src,
             dst_ref=dst,
-            send_sem=r.ss.at[len(sends)],
-            recv_sem=recv_sem(key),
+            send_sem=sem_of(r.ss, send_ids, out),
+            recv_sem=sem_of(r.rs, recv_ids, in_group or key),
             device_id=dev,
             device_id_type=MESH,
         )
         cp.start()
-        sends.append((src, dst, len(sends), key, dev))
-
-    def wait_send(entry):
-        src, dst, k, key, dev = entry
+        sends.append((src, out, key))
+
+    def wait_send(out, ref):
         pltpu.make_async_remote_copy(
-            src_ref=src,
-            dst_ref=dst,
-            send_sem=r.ss.at[k],
-            recv_sem=recv_sem(key),
-            device_id=dev,
+            src_ref=ref,
+            dst_ref=ref,
+            send_sem=sem_of(r.ss, send_ids, out),
+            recv_sem=r.rs.at[0],
+            device_id=partner,
             device_id_type=MESH,
         ).wait_send()
 
     waited = set()
 
     def wait_sent(key):
-        for entry in sends:
-            if entry[3] == key:
-                wait_send(entry)
-                waited.add(key)
+        for src, out, k in sends:
+            if k == key:
+                wait_send(out, src)
+                waited.add(out)
 
     def wait_recv(key, ref):
         pltpu.make_async_remote_copy(
             src_ref=ref,
             dst_ref=ref,
             send_sem=r.ss.at[0],
-            recv_sem=recv_sem(key),
+            recv_sem=sem_of(r.rs, recv_ids, key),
             device_id=partner,
             device_id_type=MESH,
         ).wait_recv()
@@ -237,7 +235,8 @@
 
     def forward(p, part, m, f):
         ref = wslice(p, part, m)
-        send(("ag", p, part, m ^ f), ref, ref, (ids[f], c))
+        last = ("plane", p, m // 4) if f == MV else None
+        send(("ag", p, part, m ^ f), ref, ref, (ids[f], c), ("ag", p, part), last)
 
     def got(p, part, m):
         wait_recv(("ag", p, part, m), wslice(p, part, m))
@@ -275,9 +274,7 @@
         return steps
 
     def ag_plane(p, zm):
-        for m in (4 * zm + MV, 4 * zm + MU + MV):
-            got(p, "A", m)
-            got(p, "C", m)
+        wait_recv(("plane", p, zm), wbuf(p).at[pl.ds(0, 2 * ROWS[p]), :])
 
     def run(steps):
         for s in steps:
@@ -307,7 +304,7 @@
     def rs1_send(p, zm):
         rows = 2 * ROWS[p]
         s = pl.ds(zm * rows, rows)
-        send(("r1", p, zm), r.S1[p].at[s, :], r.R1[p].at[s, :], (ids[MV], c))
+        send(("r1", p, zm), r.S1[p].at[s, :], r.R1[p].at[s, :], (ids[MV], c), ("S1", p))
 
     def rs_sum1(p, zm):
         rows, a = ROWS[p], APART[p]
@@ -322,7 +319,7 @@
             if du == 1:
                 q = pl.ds(zm * a, a)
                 r.S2A[p][q, :] = top.astype(BF)
-                send(("r2a", p, zm), r.S2A[p].at[q, :], r.R2A[p].at[q, :], (ids[MU], c))
+                send(("r2a", p, zm), r.S2A[p].at[q, :], r.R2A[p].at[q, :], (ids[MU], c), ("S2A", p))
             else:
                 g[o : o + a, :] = top
             if zm:
@@ -332,7 +329,7 @@
                 g[o + a : o + rows, :] = low
         if zm:
             q = pl.ds((zm - 1) * 2 * b, 2 * b)
-            send(("r2c", p, zm), r.S2C[p].at[q, :], r.R2C[p].at[q, :], (ids[4 * zm], c))
+            send(("r2c", p), r.S2C[p].at[q, :], r.R2C[p].at[q, :], (ids[4 * zm], c), ("S2C", p))
 
     def rs_sum2a(p, zm):
         rows, a = ROWS[p], APART[p]
@@ -344,7 +341,7 @@
         if zm:
             k = pl.ds((zm - 1) * a, a)
             r.S3A[p][k, :] = val.astype(BF)
-            send(("r3a", p, zm), r.S3A[p].at[k, :], r.R3A[p].at[k, :], (ids[4 * zm], c))
+            send(("r3a", p), r.S3A[p].at[k, :], r.R3A[p].at[k, :], (ids[4 * zm], c), ("S3A", p))
         else:
             g[o : o + a, :] = val
 
@@ -352,8 +349,7 @@
         rows, a = ROWS[p], APART[p]
         b = rows - a
         g, r2 = r.G[p], r.R2C[p]
-        for zm in (1, 2, 3):
-            wait_recv(("r2c", p, zm), r2.at[pl.ds((zm - 1) * 2 * b, 2 * b), :])
+        wait_recv(("r2c", p), r2)
         for du in (1, 0):
             o = du * rows + a
             val = g[o : o + b, :]
@@ -370,8 +366,7 @@
         rows, a = ROWS[p], APART[p]
         g = r.G[p]
         r3a, r3c = r.R3A[p], r.R3C[p]
-        for zm in (1, 2, 3):
-            wait_recv(("r3a", p, zm), r3a.at[pl.ds((zm - 1) * a, a), :])
+        wait_recv(("r3a", p), r3a)
         val = g[0:a, :]
         for zm in (1, 2, 3):
             val = val + r3a[(zm - 1) * a : zm * a, :].astype(F32)
@@ -810,9 +805,20 @@
         getattr(r, n)[...] = back[k, 0:24]
     put("dwu", "dwo", "dga", "dba", "dgf", "dbf")
 
-    for entry in sends:
-        if entry[3] not in waited:
-            wait_send(entry)
+    for src, out, key in sends:
+        if out in waited:
+            continue
+        waited.add(out)
+        if out[0] == "one":
+            ref = src
+        elif out[0] == "ag":
+            count = sum(o == out for _, o, _ in sends)
+            n_rows = APART[out[1]] if out[2] == "A" else ROWS[out[1]] - APART[out[1]]
+            ref = wbuf(out[1]).at[pl.ds(0, count * n_rows), :]
+        else:
+            ref = getattr(r, out[0])[out[1]]
+        wait_send(out, ref)
+    assert len(send_ids) == SENT and len(recv_ids) == RECEIVED, (len(send_ids), len(recv_ids))
     for cp in out_copies:
         cp.wait()
 

time: 145 us -> 143 us (0.986)
  Pallas kernels: 144 us -> 142 us
    pallas_call x1, Pallas kernels: 141 us -> 139 us  [layer_small(): pl.pallas_call(layer_kernel, out_shape=out_shape, in_specs=[smem if n in...]
where the time goes in v6:
time: 143 us
  Pallas kernels  142 us (99%)
    pallas_call x1, Pallas kernels, layer_small(): pl.pallas_call(layer_kernel, out_shape=out_shape, in_specs=[smem if n in...  139 us

profile of v6, /device:TPU:0, one launch (start us, length us, event | category | flops | bytes accessed | tf_op | source)
XLA Modules:
  0.0 142.6 jit_solution(13483932221019070685)
XLA Ops:
  0.6 139.1 %shard_map.229 = (bf16[256,768]{1,0:T(8,128)(2,1)}, bf16[256,768]{1,0:T(8,128)(2,1)}, f32[48,384]{1,0:T(8,128)}, f32[48,384]{1,0:T(8,128)}, f32[48,384]{1,0:T(8,...) custom-call(bf16[256,768]{1,0:T(8,128)(2,1)} %refs_0_.1, ...), custom_call_target="tpu_custom_call" | custom-call | tf_op jit(solution)/shard_map/pallas_call | solution.py:840
  139.8 2.6 %shard_map.230 = (bf16[256,768]{1,0:T(8,128)(2,1)}, bf16[256,768]{1,0:T(8,128)(2,1)}, f32[48,384]{1,0:T(8,128)}, f32[48,384]{1,0:T(8,128)}, f32[48,384]{1,0:T(8,...) custom-call(bf16[256,768]{1,0:T(8,128)(2,1)} %get-tuple-element.36.r, ...), custom_call_target="tpu_custom_call" | custom-call | tf_op jit(solution)/shard_map/pallas_call | solution.py:850

commit v7 on v6

--- a/solution.py
+++ b/solution.py
@@ -462,7 +462,7 @@
         [functools.partial(vec_step, 0, 2)] + u_steps[1:3],
         u_steps[3:5],
         u_steps[5:8],
-        u_steps[8:10],
+        [functools.partial(ag_own, "D")] + u_steps[8:10],
     ]
     lane = lax.broadcasted_iota(jnp.int32, (1, 128), 1)
 
@@ -500,7 +500,6 @@
     lax.fori_loop(0, 6, fwd_head, 0)
 
     send("att", r.ATT.at[:, oth_rows, :], r.ATTR, partner)
-    ag_own("D")
     for zm in range(4):
         ag_plane("O", zm)
     send("wop", r.WOP.at[c], r.WOP.at[c], partner)
@@ -824,14 +823,21 @@
 
 
 def hand_over(*refs):
-    half = len(refs) // 2
-    for src, dst in zip(refs[:half], refs[half:]):
-        dst[...] = src[...]
+    n = len(MOVED_OUT)
+    srcs, dsts, bufs, sems = refs[:n], refs[n : 2 * n], refs[2 * n : 3 * n], refs[3 * n]
+    reads = [pltpu.make_async_copy(srcs[k], bufs[k], sems.at[k]) for k in range(n)]
+    writes = [pltpu.make_async_copy(bufs[k], dsts[k], sems.at[n + k]) for k in range(n)]
+    for cp in reads:
+        cp.start()
+    for rd, wr in zip(reads, writes):
+        rd.wait()
+        wr.start()
+    for cp in writes:
+        cp.wait()
 
 
 def layer_small(*args):
     shapes = tuple((shape, dtype) for _, shape, dtype in MOVED_OUT)
-    vmem = pl.BlockSpec(memory_space=pltpu.VMEM)
     smem = pl.BlockSpec(memory_space=pltpu.SMEM)
     anywhere = pl.BlockSpec(memory_space=pl.ANY)
     out_shape = tuple(jax.ShapeDtypeStruct(s, d) for s, d in shapes)
@@ -850,8 +856,10 @@
     outs = pl.pallas_call(
         hand_over,
         out_shape=out_shape,
-        in_specs=[vmem for _ in shapes],
-        out_specs=tuple(vmem for _ in shapes),
+        in_specs=[anywhere for _ in shapes],
+        out_specs=tuple(anywhere for _ in shapes),
+        scratch_shapes=[pltpu.VMEM(shape, dtype) for shape, dtype in shapes]
+        + [pltpu.SemaphoreType.DMA((2 * len(shapes),))],
     )(*outs)
     up = OUT_NAMES.index("dwu")
     return outs[:up] + (outs[up].T,) + outs[up + 1 :]

time: 143 us -> 141 us (0.986)
  Pallas kernels: 142 us -> 140 us
where the time goes in v7:
time: 141 us
  Pallas kernels  140 us (99%)
    pallas_call x1, Pallas kernels, layer_small(): pl.pallas_call(layer_kernel, out_shape=out_shape, in_specs=[smem if n in...  138 us

profile of v7, /device:TPU:0, one launch (start us, length us, event | category | flops | bytes accessed | tf_op | source)
XLA Modules:
  0.0 141.0 jit_solution(16851869270784042201)
XLA Ops:
  0.6 137.8 %shard_map.229 = (bf16[256,768]{1,0:T(8,128)(2,1)}, bf16[256,768]{1,0:T(8,128)(2,1)}, f32[48,384]{1,0:T(8,128)}, f32[48,384]{1,0:T(8,128)}, f32[48,384]{1,0:T(8,...) custom-call(bf16[256,768]{1,0:T(8,128)(2,1)} %refs_0_.1, ...), custom_call_target="tpu_custom_call" | custom-call | tf_op jit(solution)/shard_map/pallas_call | solution.py:846
  138.4 2.4 %shard_map.230 = (bf16[256,768]{1,0:T(8,128)(2,1)}, bf16[256,768]{1,0:T(8,128)(2,1)}, f32[48,384]{1,0:T(8,128)}, f32[48,384]{1,0:T(8,128)}, f32[48,384]{1,0:T(8,...) custom-call(bf16[256,768]{1,0:T(8,128)(2,1)} %get-tuple-element.36.r, ...), custom_call_target="tpu_custom_call" | custom-call | tf_op jit(solution)/shard_map/pallas_call | solution.py:856

commit v8 on v7

--- a/solution.py
+++ b/solution.py
@@ -643,8 +643,8 @@
                 send("gn", r.SEC.at[oth_rows, :], r.SECR, partner)
         if n_done == 2:
             rs_sum1("D", 3)
+    rs1_send("D", 1)
     rs_sum1("U", 3)
-    rs1_send("D", 1)
     wait_recv("gn", r.SECR)
 
     def ln1_back(t, sums):

time: 141 us -> 141 us (level)
  no operation moved by 1% of the time
where the time goes in v8:
time: 141 us
  Pallas kernels  140 us (99%)
    pallas_call x1, Pallas kernels, layer_small(): pl.pallas_call(layer_kernel, out_shape=out_shape, in_specs=[smem if n in...  138 us

profile of v8, /device:TPU:0, one launch (start us, length us, event | category | flops | bytes accessed | tf_op | source)
XLA Modules:
  0.0 141.0 jit_solution(16425231129724927916)
XLA Ops:
  0.6 137.8 %shard_map.229 = (bf16[256,768]{1,0:T(8,128)(2,1)}, bf16[256,768]{1,0:T(8,128)(2,1)}, f32[48,384]{1,0:T(8,128)}, f32[48,384]{1,0:T(8,128)}, f32[48,384]{1,0:T(8,...) custom-call(bf16[256,768]{1,0:T(8,128)(2,1)} %refs_0_.1, ...), custom_call_target="tpu_custom_call" | custom-call | tf_op jit(solution)/shard_map/pallas_call | solution.py:846
  138.4 2.4 %shard_map.230 = (bf16[256,768]{1,0:T(8,128)(2,1)}, bf16[256,768]{1,0:T(8,128)(2,1)}, f32[48,384]{1,0:T(8,128)}, f32[48,384]{1,0:T(8,128)}, f32[48,384]{1,0:T(8,...) custom-call(bf16[256,768]{1,0:T(8,128)(2,1)} %get-tuple-element.36.r, ...), custom_call_target="tpu_custom_call" | custom-call | tf_op jit(solution)/shard_map/pallas_call | solution.py:856
